TPU v7x, 256 devices: a whole 4x4x8 slice. The times are simulated.
256 devices in a mesh: row: 8 (over y, x_lo), col: 32 (over x_hi, z, core).
Axes of the slice: x: 4 (x_hi: 2, x_lo: 2; x = x_hi * 2 + x_lo), y: 4, z: 8, core: 2. Of those that a mesh axis runs over, the one named last changes fastest.
Arguments:
- density: float32 [4096, 4096], P('row', 'col'), as said below
- pattern: int32 [32, 6], replicated, may hold values from 0 to 31, as said below
Outputs:
- purified: float32 [4096, 4096], P('row', 'col')
Inputs may be any that keep to these rules, and one draw needn't show every extreme that they name: density is symmetric. `pattern`: each row lists 6 different block columns; the first is the row's own index.
All inputs are finite; a program needn't handle non-finite values.
Results may differ from a plain program's by a relative error of at most 0.00021.
Values sent between devices are 32-bit elements; how exact they have to be, the bound alone decides.
No kernel may reach another device: no remote copies, remote signals or barrier semaphores. Data moves between devices by JAX's collectives and lax.ppermute only.
A program may use at most 64 MiB of HBM per device.

v0:
```python
import jax
import jax.numpy as jnp
from jax import lax
from jax.experimental import pallas as pl
from jax.experimental.pallas import tpu as pltpu
from jax.sharding import PartitionSpec as P

BLK = 128
NNZ = 6
ITERS = 2
X_HI, Z, CORE = 2, 8, 2
Y, X_LO = 4, 2
GROUP = 4


def col_id(x_hi, z, core):
    return (x_hi * Z + z % Z) * CORE + core


COLS = [(x, z, c) for x in range(X_HI) for z in range(Z) for c in range(CORE)]
UP = [(col_id(x, z, c), col_id(x, z + 1, c)) for x, z, c in COLS]
DOWN = [(col_id(x, z, c), col_id(x, z - 1, c)) for x, z, c in COLS]
ACROSS = [(col_id(x, z, c), col_id(1 - x, z, c)) for x, z, c in COLS]
TWIN = [(col_id(x, z, c), col_id(x, z, 1 - c)) for x, z, c in COLS]
ROWS = [(y, x) for y in range(Y) for x in range(X_LO)]
NORTH = [(y * X_LO + x, (y + 1) % Y * X_LO + x) for y, x in ROWS]
SOUTH = [(y * X_LO + x, (y - 1) % Y * X_LO + x) for y, x in ROWS]
OPPOSITE = [(y * X_LO + x, (y + 2) % Y * X_LO + x) for y, x in ROWS]
BESIDE = [(y * X_LO + x, y * X_LO + 1 - x) for y, x in ROWS]


def send(v, pairs):
    return lax.ppermute(v, "col", pairs)


def gather_rows(tile):
    move = lambda v, pairs: lax.ppermute(v, "row", pairs)
    first = move(tile, BESIDE), move(tile, NORTH), move(tile, SOUTH)
    beside, south, north = lax.optimization_barrier(first)
    return [
        tile, beside, south, north,
        move(south, BESIDE), move(north, BESIDE), move(south, NORTH), move(beside, OPPOSITE),
    ]


def row_places(row):
    y, x_lo = row // X_LO, row % X_LO
    away = jnp.array([0, 0, -1, 1, -1, 1, 2, 2], jnp.int32)
    beside = jnp.array([0, 1, 0, 0, 1, 1, 0, 1], jnp.int32)
    return (y + away + Y) % Y * X_LO + (x_lo + beside) % X_LO


def gather_cols(tile):
    other = send(tile, ACROSS)
    pieces = [tile, other]
    up, down, other_up, other_down = tile, tile, other, other
    for _ in range(3):
        up, down = send(up, UP), send(down, DOWN)
        other_up, other_down = send(other_up, UP), send(other_down, DOWN)
        pieces += [up, down, other_up, other_down]
    return pieces + [send(up, UP), send(other_down, DOWN)]


def col_places(col):
    x_hi, z = col // (Z * CORE), (col // CORE) % Z
    away = jnp.array([0, 0, -1, 1, -1, 1, -2, 2, -2, 2, -3, 3, -3, 3, 4, 4], jnp.int32)
    across = jnp.array([0, 1, 0, 0, 1, 1, 0, 0, 1, 1, 0, 0, 1, 1, 0, 1], jnp.int32)
    return (x_hi + across) % X_HI * Z + (z + away + Z) % Z


def to_pair(tile, core):
    rows = tile.reshape(-1, CORE, BLK, BLK)
    mine = jnp.where(core == 0, rows[:, 0], rows[:, 1])
    other = send(jnp.where(core == 0, rows[:, 1], rows[:, 0]), TWIN)
    left = jnp.where(core == 0, mine, other)
    right = jnp.where(core == 0, other, mine)
    return jnp.concatenate([left, right], axis=2).reshape(-1, CORE * BLK)


def split(x):
    high = x.astype(jnp.bfloat16)
    return high, (x - high.astype(jnp.float32)).astype(jnp.bfloat16)


def partial_product(where, lefts, rights, high, low, total):
    rows = rights[0].shape[0]
    for j, piece in enumerate(rights):
        to = pl.ds(pl.multiple_of(where[len(lefts) + j] * rows, BLK), rows)
        high[to, :], low[to, :] = split(piece[...])
    dot = lambda a, b: jnp.dot(a, b, preferred_element_type=jnp.float32)
    for g in range(0, len(lefts), GROUP):
        slots = range(g, g + GROUP)
        left_high, left_low = split(jnp.concatenate([lefts[s][...] for s in slots], axis=1))
        at = [pl.ds(pl.multiple_of(where[s] * BLK, BLK), BLK) for s in slots]
        right_high = jnp.concatenate([high[i, :] for i in at], axis=0)
        right_low = jnp.concatenate([low[i, :] for i in at], axis=0)
        term = (dot(left_high, right_low) + dot(left_low, right_high)) + dot(left_high, right_high)
        total[...] = term if g == 0 else total[...] + term


def mask_pair(block, live, i):
    return jnp.concatenate(
        [live[CORE * i + c] * block[:, c * BLK : (c + 1) * BLK] for c in range(CORE)], axis=1
    )


def square_body(lefts, rights, where, live, *refs):
    left, right = refs[:lefts], refs[lefts : lefts + rights]
    keep, give, *scratch = refs[lefts + rights :]
    partial_product(where, left, right, *scratch)
    total = scratch[-1]
    core = where[lefts + rights]
    for q in range(keep.shape[0] // BLK):
        for out, i in ((keep, CORE * q + core), (give, CORE * q + 1 - core)):
            block = total[pl.ds(pl.multiple_of(i * BLK, BLK), BLK), :]
            out[pl.ds(q * BLK, BLK), :] = mask_pair(block, live, i)


def step_body(lefts, rights, where, live, *refs):
    left, right = refs[:lefts], refs[lefts : lefts + rights]
    kept, given, keep, give, *scratch = refs[lefts + rights :]
    partial_product(where, left, right, *scratch)
    total = scratch[-1]
    core = where[lefts + rights]
    first = core == 0
    for i in range(keep.shape[0] // BLK):
        rows = pl.ds(i * BLK, BLK)
        q = pl.ds(i // CORE * BLK, BLK)
        square = jnp.where(core == i % CORE, kept[q, :], given[q, :])
        part = 3.0 * square - 2.0 * mask_pair(total[rows, :], live, i)
        keep[rows, :] = jnp.where(first, part[:, :BLK], part[:, BLK:])
        give[rows, :] = jnp.where(first, part[:, BLK:], part[:, :BLK])


def call(body, where, live, left, right, extra, shape):
    rows, width = left[0].shape[0], right[0].shape[1]
    depth = len(left) * BLK
    vmem = pl.BlockSpec(memory_space=pltpu.VMEM)
    out = jax.ShapeDtypeStruct(shape, jnp.float32)
    return pl.pallas_call(
        lambda *refs: body(len(left), len(right), *refs),
        out_shape=(out, out),
        in_specs=[pl.BlockSpec(memory_space=pltpu.SMEM)] * 2
        + [vmem] * (len(left) + len(right) + len(extra)),
        out_specs=(vmem, vmem),
        scratch_shapes=[
            pltpu.VMEM((depth, width), jnp.bfloat16),
            pltpu.VMEM((depth, width), jnp.bfloat16),
            pltpu.VMEM((rows, width), jnp.float32),
        ],
        compiler_params=pltpu.CompilerParams(vmem_limit_bytes=16 << 20),
        cost_estimate=pl.CostEstimate(
            flops=6 * rows * depth * width,
            bytes_accessed=4 * (depth * (rows + width) + 2 * rows * width),
            transcendentals=0,
        ),
    )(where, live, *left, *right, *extra)


def local(density, pattern):
    rows_dev, cols_dev = density.shape
    row_number = lax.axis_index("row")
    col_index = lax.axis_index("col")
    core = col_index % CORE
    block_count = cols_dev * lax.axis_size("col") // BLK
    row_blocks = rows_dev // BLK
    listed = jnp.any(
        pattern[:, :, None] == jnp.arange(block_count, dtype=jnp.int32)[None, None, :], axis=1
    ).astype(jnp.float32)
    block_live = jnp.maximum(listed, listed.T)
    my_rows = lax.dynamic_slice_in_dim(block_live, row_number * row_blocks, row_blocks, 0)
    chip = lax.dynamic_slice_in_dim(my_rows, col_index - core, CORE, 1)
    tile_live = jnp.where(core == 0, chip[:, 0], chip[:, 1])
    tile_mask = jnp.repeat(tile_live, BLK)[:, None]
    live = chip.reshape(-1)
    global_rows = row_number * rows_dev + jnp.arange(rows_dev, dtype=jnp.int32)
    global_cols = col_index * cols_dev + jnp.arange(cols_dev, dtype=jnp.int32)
    identity = (global_rows[:, None] == global_cols[None, :]).astype(jnp.float32)
    current = 0.5 * identity + 0.45 / jnp.sqrt(jnp.float32(2 * NNZ * BLK)) * tile_mask * density
    where = jnp.concatenate(
        [col_places(col_index), row_places(row_number), core[None]]
    ).astype(jnp.int32)
    def purify(_, current):
        left = gather_cols(current)
        right = gather_rows(to_pair(current, core))
        kept, given = call(
            square_body, where, live, left, right, [], (rows_dev // CORE, CORE * BLK)
        )
        square = gather_rows(kept + send(given, TWIN))
        keep, give = call(
            step_body, where, live, left, square, [kept, given], (rows_dev, BLK)
        )
        return keep + send(give, TWIN)

    return lax.fori_loop(0, ITERS, purify, current)


def solution(mesh):
    return jax.shard_map(
        local,
        mesh=mesh,
        in_specs=(P("row", "col"), P()),
        out_specs=P("row", "col"),
        check_vma=False,
    )
```

profile of v0, /device:TPU:1, one launch (start us, length us, event | category | flops | bytes accessed | tf_op | source)
XLA Modules:
  0.0 188.0 jit_solution(15655464713142804879)
XLA Ops:
  3.8 183.5 %while.12 = (s32[]{:T(128)}, f32[512,128]{1,0:T(8,128)S(1)}, pred[]{:T(512)}, s32[25]{0:T(128)S(1)}, f32[8]{0:T(128)S(1)}, /*index=5*/s32[]{:T(128)}) while((s32[]{:T(128)}, f32[512,128]{1,0:T(8,128)S(1)}, pred[]{:T(512)}, s32[25]{0:T(128)S(1)}, f32[8]{0:T(128)S(1)}, /*index=5*/s32[]{:T(128)}) %tuple.35), condition=%wide.region_2.3_spmd, body=%wide.region_1.2_spmd.sunk | while | flops 3221553152 | bytes 50858308 | solution.py:195
  3.9 3.3 %collective-permute-start.15 = (f32[2,128,128]{2,1,0:T(8,128)S(1)}, f32[2,128,128]{2,1,0:T(8,128)S(1)}, u32[]{:S(2)}, u32[]{:S(2)}) collective-permute-start(f32[2,128,128]{2,1,0:T(8,128)S(1)} %select_bitcast_fusion.2), channel_id=1, source_target_pairs={{0,1},{1,0},{2,3},{3,2},{4,5},{5,4},{6,7},{7,6},{8,9},{9,8},{10,11... | collective-permute-start | bytes 393224 | tf_op jit(solution)/shard_map/while/body/eval_jaxpr/ppermute | solution.py:33
  7.2 3.9 %collective-permute-start.2 = (f32[512,128]{1,0:T(8,128)S(1)}, f32[512,128]{1,0:T(8,128)S(1)}, u32[]{:S(2)}, u32[]{:S(2)}) collective-permute-start(f32[512,128]{1,0:T(8,128)S(1)} %get-tuple-element.150.refs_2_), channel_id=1, source_target_pairs={{0,14},{1,15},{2,0},{3,1},{4,2},{5,3},{6,4},{7,5},{8,6},{9,7},{10,... | collective-permute-start | bytes 786440 | tf_op jit(solution)/shard_map/while/body/eval_jaxpr/ppermute | solution.py:33
  13.8 2.8 %collective-permute-start.18 = (f32[256,256]{1,0:T(8,128)S(1)}, f32[256,256]{1,0:T(8,128)S(1)}, u32[]{:S(2)}, u32[]{:S(2)}) collective-permute-start(f32[256,256]{1,0:T(8,128)S(1)} %bitcast.50), channel_id=1, source_target_pairs={{0,192},{32,224},{64,0},{96,32},{128,64},{160,96},{192,128},{224,1... | collective-permute-start | bytes 786440 | tf_op jit(solution)/shard_map/while/body/eval_jaxpr/ppermute | solution.py:37
  25.8 2.9 %collective-permute-start.22 = (f32[256,256]{1,0:T(8,128)S(1)}, f32[256,256]{1,0:T(8,128)S(1)}, u32[]{:S(2)}, u32[]{:S(2)}) collective-permute-start(f32[256,256]{1,0:T(8,128)S(1)} %collective-permute-done.16.refs_19_), channel_id=1, source_target_pairs={{0,128},{32,160},{64,192},{96,224},{128,0},{160,32},{192,64},{224,... | collective-permute-start | bytes 786440 | tf_op jit(solution)/shard_map/while/body/eval_jaxpr/ppermute | solution.py:37
  37.9 3.2 %collective-permute-start.12 = (f32[512,128]{1,0:T(8,128)S(1)}, f32[512,128]{1,0:T(8,128)S(1)}, u32[]{:S(2)}, u32[]{:S(2)}) collective-permute-start(f32[512,128]{1,0:T(8,128)S(1)} %collective-permute-done.8.refs_11_), channel_id=1, source_target_pairs={{0,14},{1,15},{2,0},{3,1},{4,2},{5,3},{6,4},{7,5},{8,6},{9,7},{10,... | collective-permute-start | bytes 786440 | tf_op jit(solution)/shard_map/while/body/eval_jaxpr/ppermute | solution.py:33
  43.9 4.0 %collective-permute-done.7.refs_10_ = f32[512,128]{1,0:T(8,128)S(1)} collective-permute-done((f32[512,128]{1,0:T(8,128)S(1)}, f32[512,128]{1,0:T(8,128)S(1)}, u32[]{:S(2)}, u32[]{:S(2)}) %collective-permute-start.7) | collective-permute-done | bytes 262176 | tf_op jit(solution)/shard_map/while/body/eval_jaxpr/ppermute | solution.py:33
  53.5 5.6 %collective-permute-done.11.refs_14_ = f32[512,128]{1,0:T(8,128)S(1)} collective-permute-done((f32[512,128]{1,0:T(8,128)S(1)}, f32[512,128]{1,0:T(8,128)S(1)}, u32[]{:S(2)}, u32[]{:S(2)}) %collective-permute-start.11) | collective-permute-done | bytes 262176 | tf_op jit(solution)/shard_map/while/body/eval_jaxpr/ppermute | solution.py:33
  59.1 2.8 %eval_jaxpr.6 = (f32[256,256]{1,0:T(8,128)S(1)}, f32[256,256]{1,0:T(8,128)S(1)}) custom-call(s32[25]{0:T(128)S(1)} %get-tuple-element.158.refs_0_, f32[8]{0:T(128)S(1)} %get-tuple-element.159.refs_1_, f32[512,128]{1,0:T(8,128)S(1)} %get-tuple-element.150.refs_2_, f32[512,128]{1,0:T(8,128)S(1)} %collective-permute-done.refs_3_, ...), custom_call_target="tpu_custom_call" | custom-call | flops 1610612736 | bytes 7340032 | tf_op jit(solution)/shard_map/while/body/eval_jaxpr/pallas_call | solution.py:140
  61.9 4.8 %collective-permute-start.23 = (f32[256,256]{1,0:T(8,128)S(1)}, f32[256,256]{1,0:T(8,128)S(1)}, u32[]{:S(2)}, u32[]{:S(2)}) collective-permute-start(f32[256,256]{1,0:T(8,128)S(1)} %get-tuple-element.137.refs_27_), channel_id=1, source_target_pairs={{0,1},{1,0},{2,3},{3,2},{4,5},{5,4},{6,7},{7,6},{8,9},{9,8},{10,11... | collective-permute-start | bytes 786440 | tf_op jit(solution)/shard_map/while/body/eval_jaxpr/ppermute | solution.py:33
  70.3 5.2 %collective-permute-done.26.refs_21_ = f32[256,256]{1,0:T(8,128)S(1)} collective-permute-done((f32[256,256]{1,0:T(8,128)S(1)}, f32[256,256]{1,0:T(8,128)S(1)}, u32[]{:S(2)}, u32[]{:S(2)}) %collective-permute-start.26) | collective-permute-done | bytes 262176 | tf_op jit(solution)/shard_map/while/body/eval_jaxpr/ppermute | solution.py:37
  80.9 4.6 %collective-permute-done.30.refs_25_ = f32[256,256]{1,0:T(8,128)S(1)} collective-permute-done((f32[256,256]{1,0:T(8,128)S(1)}, f32[256,256]{1,0:T(8,128)S(1)}, u32[]{:S(2)}, u32[]{:S(2)}) %collective-permute-start.30) | collective-permute-done | bytes 262176 | tf_op jit(solution)/shard_map/while/body/eval_jaxpr/ppermute | solution.py:37
  85.6 7.0 %collective-permute-done.29.refs_24_ = f32[256,256]{1,0:T(8,128)S(1)} collective-permute-done((f32[256,256]{1,0:T(8,128)S(1)}, f32[256,256]{1,0:T(8,128)S(1)}, u32[]{:S(2)}, u32[]{:S(2)}) %collective-permute-start.29) | collective-permute-done | bytes 262176 | tf_op jit(solution)/shard_map/while/body/eval_jaxpr/ppermute | solution.py:37
  98.2 3.0 %collective-permute-start.2 = (f32[512,128]{1,0:T(8,128)S(1)}, f32[512,128]{1,0:T(8,128)S(1)}, u32[]{:S(2)}, u32[]{:S(2)}) collective-permute-start(f32[512,128]{1,0:T(8,128)S(1)} %get-tuple-element.150.refs_2_), channel_id=1, source_target_pairs={{0,14},{1,15},{2,0},{3,1},{4,2},{5,3},{6,4},{7,5},{8,6},{9,7},{10,... | collective-permute-start | bytes 786440 | tf_op jit(solution)/shard_map/while/body/eval_jaxpr/ppermute | solution.py:33
  127.8 3.2 %collective-permute-start.12 = (f32[512,128]{1,0:T(8,128)S(1)}, f32[512,128]{1,0:T(8,128)S(1)}, u32[]{:S(2)}, u32[]{:S(2)}) collective-permute-start(f32[512,128]{1,0:T(8,128)S(1)} %collective-permute-done.8.refs_11_), channel_id=1, source_target_pairs={{0,14},{1,15},{2,0},{3,1},{4,2},{5,3},{6,4},{7,5},{8,6},{9,7},{10,... | collective-permute-start | bytes 786440 | tf_op jit(solution)/shard_map/while/body/eval_jaxpr/ppermute | solution.py:33
  133.3 3.7 %collective-permute-done.7.refs_10_ = f32[512,128]{1,0:T(8,128)S(1)} collective-permute-done((f32[512,128]{1,0:T(8,128)S(1)}, f32[512,128]{1,0:T(8,128)S(1)}, u32[]{:S(2)}, u32[]{:S(2)}) %collective-permute-start.7) | collective-permute-done | bytes 262176 | tf_op jit(solution)/shard_map/while/body/eval_jaxpr/ppermute | solution.py:33
  139.8 2.8 %collective-permute-done.13.refs_16_ = f32[512,128]{1,0:T(8,128)S(1)} collective-permute-done((f32[512,128]{1,0:T(8,128)S(1)}, f32[512,128]{1,0:T(8,128)S(1)}, u32[]{:S(2)}, u32[]{:S(2)}) %collective-permute-start.13) | collective-permute-done | bytes 262176 | tf_op jit(solution)/shard_map/while/body/eval_jaxpr/ppermute | solution.py:33
  142.6 5.4 %collective-permute-done.11.refs_14_ = f32[512,128]{1,0:T(8,128)S(1)} collective-permute-done((f32[512,128]{1,0:T(8,128)S(1)}, f32[512,128]{1,0:T(8,128)S(1)}, u32[]{:S(2)}, u32[]{:S(2)}) %collective-permute-start.11) | collective-permute-done | bytes 262176 | tf_op jit(solution)/shard_map/while/body/eval_jaxpr/ppermute | solution.py:33
  148.0 2.8 %eval_jaxpr.6 = (f32[256,256]{1,0:T(8,128)S(1)}, f32[256,256]{1,0:T(8,128)S(1)}) custom-call(s32[25]{0:T(128)S(1)} %get-tuple-element.158.refs_0_, f32[8]{0:T(128)S(1)} %get-tuple-element.159.refs_1_, f32[512,128]{1,0:T(8,128)S(1)} %get-tuple-element.150.refs_2_, f32[512,128]{1,0:T(8,128)S(1)} %collective-permute-done.refs_3_, ...), custom_call_target="tpu_custom_call" | custom-call | flops 1610612736 | bytes 7340032 | tf_op jit(solution)/shard_map/while/body/eval_jaxpr/pallas_call | solution.py:140
  150.8 4.4 %collective-permute-start.23 = (f32[256,256]{1,0:T(8,128)S(1)}, f32[256,256]{1,0:T(8,128)S(1)}, u32[]{:S(2)}, u32[]{:S(2)}) collective-permute-start(f32[256,256]{1,0:T(8,128)S(1)} %get-tuple-element.137.refs_27_), channel_id=1, source_target_pairs={{0,1},{1,0},{2,3},{3,2},{4,5},{5,4},{6,7},{7,6},{8,9},{9,8},{10,11... | collective-permute-start | bytes 786440 | tf_op jit(solution)/shard_map/while/body/eval_jaxpr/ppermute | solution.py:33
  159.7 4.6 %collective-permute-done.26.refs_21_ = f32[256,256]{1,0:T(8,128)S(1)} collective-permute-done((f32[256,256]{1,0:T(8,128)S(1)}, f32[256,256]{1,0:T(8,128)S(1)}, u32[]{:S(2)}, u32[]{:S(2)}) %collective-permute-start.26) | collective-permute-done | bytes 262176 | tf_op jit(solution)/shard_map/while/body/eval_jaxpr/ppermute | solution.py:37
  164.3 3.1 %collective-permute-done.25.refs_20_ = f32[256,256]{1,0:T(8,128)S(1)} collective-permute-done((f32[256,256]{1,0:T(8,128)S(1)}, f32[256,256]{1,0:T(8,128)S(1)}, u32[]{:S(2)}, u32[]{:S(2)}) %collective-permute-start.25) | collective-permute-done | bytes 262176 | tf_op jit(solution)/shard_map/while/body/eval_jaxpr/ppermute | solution.py:37
  170.6 4.6 %collective-permute-done.30.refs_25_ = f32[256,256]{1,0:T(8,128)S(1)} collective-permute-done((f32[256,256]{1,0:T(8,128)S(1)}, f32[256,256]{1,0:T(8,128)S(1)}, u32[]{:S(2)}, u32[]{:S(2)}) %collective-permute-start.30) | collective-permute-done | bytes 262176 | tf_op jit(solution)/shard_map/while/body/eval_jaxpr/ppermute | solution.py:37
  175.2 7.5 %collective-permute-done.29.refs_24_ = f32[256,256]{1,0:T(8,128)S(1)} collective-permute-done((f32[256,256]{1,0:T(8,128)S(1)}, f32[256,256]{1,0:T(8,128)S(1)}, u32[]{:S(2)}, u32[]{:S(2)}) %collective-permute-start.29) | collective-permute-done | bytes 262176 | tf_op jit(solution)/shard_map/while/body/eval_jaxpr/ppermute | solution.py:37
  (146 shorter events, 92.5 us)
Async XLA Ops:
  3.9 9.9 %collective-permute-start.15 = (f32[2,128,128]{2,1,0:T(8,128)S(1)}, f32[2,128,128]{2,1,0:T(8,128)S(1)}, u32[]{:S(2)}, u32[]{:S(2)}) collective-permute-start(f32[2,128,128]{2,1,0:T(8,128)S(1)} %select_bitcast_fusion.2), channel_id=1, source_target_pairs={{0,1},{1,0},{2,3},{3,2},{4,5},{5,4},{6,7},{7,6},{8,9},{9,8},{10,11... | collective-permute-start | bytes 393224 | tf_op jit(solution)/shard_map/while/body/eval_jaxpr/ppermute | solution.py:33
  11.0 11.4 %collective-permute-start.1 = (f32[512,128]{1,0:T(8,128)S(1)}, f32[512,128]{1,0:T(8,128)S(1)}, u32[]{:S(2)}, u32[]{:S(2)}) collective-permute-start(f32[512,128]{1,0:T(8,128)S(1)} %get-tuple-element.150.refs_2_), channel_id=1, source_target_pairs={{0,2},{1,3},{2,4},{3,5},{4,6},{5,7},{6,8},{7,9},{8,10},{9,11},{10,... | collective-permute-start | bytes 786440 | tf_op jit(solution)/shard_map/while/body/eval_jaxpr/ppermute | solution.py:33
  22.4 9.9 %collective-permute-start.6 = (f32[512,128]{1,0:T(8,128)S(1)}, f32[512,128]{1,0:T(8,128)S(1)}, u32[]{:S(2)}, u32[]{:S(2)}) collective-permute-start(f32[512,128]{1,0:T(8,128)S(1)} %collective-permute-done.2.refs_5_), channel_id=1, source_target_pairs={{0,14},{1,15},{2,0},{3,1},{4,2},{5,3},{6,4},{7,5},{8,6},{9,7},{10,... | collective-permute-start | bytes 786440 | tf_op jit(solution)/shard_map/while/body/eval_jaxpr/ppermute | solution.py:33
  22.5 14.2 %collective-permute-start.3 = (f32[512,128]{1,0:T(8,128)S(1)}, f32[512,128]{1,0:T(8,128)S(1)}, u32[]{:S(2)}, u32[]{:S(2)}) collective-permute-start(f32[512,128]{1,0:T(8,128)S(1)} %collective-permute-done.refs_3_), channel_id=1, source_target_pairs={{0,2},{1,3},{2,4},{3,5},{4,6},{5,7},{6,8},{7,9},{8,10},{9,11},{10,... | collective-permute-start | bytes 786440 | tf_op jit(solution)/shard_map/while/body/eval_jaxpr/ppermute | solution.py:33
  24.8 10.6 %collective-permute-start.5 = (f32[512,128]{1,0:T(8,128)S(1)}, f32[512,128]{1,0:T(8,128)S(1)}, u32[]{:S(2)}, u32[]{:S(2)}) collective-permute-start(f32[512,128]{1,0:T(8,128)S(1)} %collective-permute-done.1.refs_4_), channel_id=1, source_target_pairs={{0,2},{1,3},{2,4},{3,5},{4,6},{5,7},{6,8},{7,9},{8,10},{9,11},{10,... | collective-permute-start | bytes 786440 | tf_op jit(solution)/shard_map/while/body/eval_jaxpr/ppermute | solution.py:33
  25.8 10.9 %collective-permute-start.22 = (f32[256,256]{1,0:T(8,128)S(1)}, f32[256,256]{1,0:T(8,128)S(1)}, u32[]{:S(2)}, u32[]{:S(2)}) collective-permute-start(f32[256,256]{1,0:T(8,128)S(1)} %collective-permute-done.16.refs_19_), channel_id=1, source_target_pairs={{0,128},{32,160},{64,192},{96,224},{128,0},{160,32},{192,64},{224,... | collective-permute-start | bytes 786440 | tf_op jit(solution)/shard_map/while/body/eval_jaxpr/ppermute | solution.py:37
  36.7 11.2 %collective-permute-start.7 = (f32[512,128]{1,0:T(8,128)S(1)}, f32[512,128]{1,0:T(8,128)S(1)}, u32[]{:S(2)}, u32[]{:S(2)}) collective-permute-start(f32[512,128]{1,0:T(8,128)S(1)} %collective-permute-done.3.refs_6_), channel_id=1, source_target_pairs={{0,2},{1,3},{2,4},{3,5},{4,6},{5,7},{6,8},{7,9},{8,10},{9,11},{10,... | collective-permute-start | bytes 786440 | tf_op jit(solution)/shard_map/while/body/eval_jaxpr/ppermute | solution.py:33
  37.9 9.9 %collective-permute-start.12 = (f32[512,128]{1,0:T(8,128)S(1)}, f32[512,128]{1,0:T(8,128)S(1)}, u32[]{:S(2)}, u32[]{:S(2)}) collective-permute-start(f32[512,128]{1,0:T(8,128)S(1)} %collective-permute-done.8.refs_11_), channel_id=1, source_target_pairs={{0,14},{1,15},{2,0},{3,1},{4,2},{5,3},{6,4},{7,5},{8,6},{9,7},{10,... | collective-permute-start | bytes 786440 | tf_op jit(solution)/shard_map/while/body/eval_jaxpr/ppermute | solution.py:33
  43.4 10.1 %collective-permute-start.13 = (f32[512,128]{1,0:T(8,128)S(1)}, f32[512,128]{1,0:T(8,128)S(1)}, u32[]{:S(2)}, u32[]{:S(2)}) collective-permute-start(f32[512,128]{1,0:T(8,128)S(1)} %collective-permute-done.9.refs_12_), channel_id=1, source_target_pairs={{0,2},{1,3},{2,4},{3,5},{4,6},{5,7},{6,8},{7,9},{8,10},{9,11},{10,... | collective-permute-start | bytes 786440 | tf_op jit(solution)/shard_map/while/body/eval_jaxpr/ppermute | solution.py:33
  47.8 11.2 %collective-permute-start.11 = (f32[512,128]{1,0:T(8,128)S(1)}, f32[512,128]{1,0:T(8,128)S(1)}, u32[]{:S(2)}, u32[]{:S(2)}) collective-permute-start(f32[512,128]{1,0:T(8,128)S(1)} %collective-permute-done.7.refs_10_), channel_id=1, source_target_pairs={{0,2},{1,3},{2,4},{3,5},{4,6},{5,7},{6,8},{7,9},{8,10},{9,11},{10,... | collective-permute-start | bytes 786440 | tf_op jit(solution)/shard_map/while/body/eval_jaxpr/ppermute | solution.py:33
  47.8 11.2 %collective-permute-start.14 = (f32[512,128]{1,0:T(8,128)S(1)}, f32[512,128]{1,0:T(8,128)S(1)}, u32[]{:S(2)}, u32[]{:S(2)}) collective-permute-start(f32[512,128]{1,0:T(8,128)S(1)} %collective-permute-done.12.refs_15_), channel_id=1, source_target_pairs={{0,14},{1,15},{2,0},{3,1},{4,2},{5,3},{6,4},{7,5},{8,6},{9,7},{10,... | collective-permute-start | bytes 786440 | tf_op jit(solution)/shard_map/while/body/eval_jaxpr/ppermute | solution.py:33
  79.8 12.8 %collective-permute-start.29 = (f32[256,256]{1,0:T(8,128)S(1)}, f32[256,256]{1,0:T(8,128)S(1)}, u32[]{:S(2)}, u32[]{:S(2)}) collective-permute-start(f32[256,256]{1,0:T(8,128)S(1)} %collective-permute-done.25.refs_20_), channel_id=1, source_target_pairs={{0,64},{32,96},{64,128},{96,160},{128,192},{160,224},{192,0},{224,... | collective-permute-start | bytes 786440 | tf_op jit(solution)/shard_map/while/body/eval_jaxpr/ppermute | solution.py:37
  80.4 12.2 %collective-permute-start.27 = (f32[256,256]{1,0:T(8,128)S(1)}, f32[256,256]{1,0:T(8,128)S(1)}, u32[]{:S(2)}, u32[]{:S(2)}) collective-permute-start(f32[256,256]{1,0:T(8,128)S(1)} %collective-permute-done.25.refs_20_), channel_id=1, source_target_pairs={{0,32},{32,0},{64,96},{96,64},{128,160},{160,128},{192,224},{224,1... | collective-permute-start | bytes 786440 | tf_op jit(solution)/shard_map/while/body/eval_jaxpr/ppermute | solution.py:37
  101.1 11.3 %collective-permute-start.1 = (f32[512,128]{1,0:T(8,128)S(1)}, f32[512,128]{1,0:T(8,128)S(1)}, u32[]{:S(2)}, u32[]{:S(2)}) collective-permute-start(f32[512,128]{1,0:T(8,128)S(1)} %get-tuple-element.150.refs_2_), channel_id=1, source_target_pairs={{0,2},{1,3},{2,4},{3,5},{4,6},{5,7},{6,8},{7,9},{8,10},{9,11},{10,... | collective-permute-start | bytes 786440 | tf_op jit(solution)/shard_map/while/body/eval_jaxpr/ppermute | solution.py:33
  112.4 9.8 %collective-permute-start.6 = (f32[512,128]{1,0:T(8,128)S(1)}, f32[512,128]{1,0:T(8,128)S(1)}, u32[]{:S(2)}, u32[]{:S(2)}) collective-permute-start(f32[512,128]{1,0:T(8,128)S(1)} %collective-permute-done.2.refs_5_), channel_id=1, source_target_pairs={{0,14},{1,15},{2,0},{3,1},{4,2},{5,3},{6,4},{7,5},{8,6},{9,7},{10,... | collective-permute-start | bytes 786440 | tf_op jit(solution)/shard_map/while/body/eval_jaxpr/ppermute | solution.py:33
  112.5 13.0 %collective-permute-start.3 = (f32[512,128]{1,0:T(8,128)S(1)}, f32[512,128]{1,0:T(8,128)S(1)}, u32[]{:S(2)}, u32[]{:S(2)}) collective-permute-start(f32[512,128]{1,0:T(8,128)S(1)} %collective-permute-done.refs_3_), channel_id=1, source_target_pairs={{0,2},{1,3},{2,4},{3,5},{4,6},{5,7},{6,8},{7,9},{8,10},{9,11},{10,... | collective-permute-start | bytes 786440 | tf_op jit(solution)/shard_map/while/body/eval_jaxpr/ppermute | solution.py:33
  113.9 11.4 %collective-permute-start.5 = (f32[512,128]{1,0:T(8,128)S(1)}, f32[512,128]{1,0:T(8,128)S(1)}, u32[]{:S(2)}, u32[]{:S(2)}) collective-permute-start(f32[512,128]{1,0:T(8,128)S(1)} %collective-permute-done.1.refs_4_), channel_id=1, source_target_pairs={{0,2},{1,3},{2,4},{3,5},{4,6},{5,7},{6,8},{7,9},{8,10},{9,11},{10,... | collective-permute-start | bytes 786440 | tf_op jit(solution)/shard_map/while/body/eval_jaxpr/ppermute | solution.py:33
  115.8 9.7 %collective-permute-start.22 = (f32[256,256]{1,0:T(8,128)S(1)}, f32[256,256]{1,0:T(8,128)S(1)}, u32[]{:S(2)}, u32[]{:S(2)}) collective-permute-start(f32[256,256]{1,0:T(8,128)S(1)} %collective-permute-done.16.refs_19_), channel_id=1, source_target_pairs={{0,128},{32,160},{64,192},{96,224},{128,0},{160,32},{192,64},{224,... | collective-permute-start | bytes 786440 | tf_op jit(solution)/shard_map/while/body/eval_jaxpr/ppermute | solution.py:37
  117.3 10.6 %collective-permute-start.8 = (f32[512,128]{1,0:T(8,128)S(1)}, f32[512,128]{1,0:T(8,128)S(1)}, u32[]{:S(2)}, u32[]{:S(2)}) collective-permute-start(f32[512,128]{1,0:T(8,128)S(1)} %collective-permute-done.4.refs_7_), channel_id=1, source_target_pairs={{0,14},{1,15},{2,0},{3,1},{4,2},{5,3},{6,4},{7,5},{8,6},{9,7},{10,... | collective-permute-start | bytes 786440 | tf_op jit(solution)/shard_map/while/body/eval_jaxpr/ppermute | solution.py:33
  125.5 11.5 %collective-permute-start.7 = (f32[512,128]{1,0:T(8,128)S(1)}, f32[512,128]{1,0:T(8,128)S(1)}, u32[]{:S(2)}, u32[]{:S(2)}) collective-permute-start(f32[512,128]{1,0:T(8,128)S(1)} %collective-permute-done.3.refs_6_), channel_id=1, source_target_pairs={{0,2},{1,3},{2,4},{3,5},{4,6},{5,7},{6,8},{7,9},{8,10},{9,11},{10,... | collective-permute-start | bytes 786440 | tf_op jit(solution)/shard_map/while/body/eval_jaxpr/ppermute | solution.py:33
  137.0 11.0 %collective-permute-start.11 = (f32[512,128]{1,0:T(8,128)S(1)}, f32[512,128]{1,0:T(8,128)S(1)}, u32[]{:S(2)}, u32[]{:S(2)}) collective-permute-start(f32[512,128]{1,0:T(8,128)S(1)} %collective-permute-done.7.refs_10_), channel_id=1, source_target_pairs={{0,2},{1,3},{2,4},{3,5},{4,6},{5,7},{6,8},{7,9},{8,10},{9,11},{10,... | collective-permute-start | bytes 786440 | tf_op jit(solution)/shard_map/while/body/eval_jaxpr/ppermute | solution.py:33
  137.0 11.0 %collective-permute-start.14 = (f32[512,128]{1,0:T(8,128)S(1)}, f32[512,128]{1,0:T(8,128)S(1)}, u32[]{:S(2)}, u32[]{:S(2)}) collective-permute-start(f32[512,128]{1,0:T(8,128)S(1)} %collective-permute-done.12.refs_15_), channel_id=1, source_target_pairs={{0,14},{1,15},{2,0},{3,1},{4,2},{5,3},{6,4},{7,5},{8,6},{9,7},{10,... | collective-permute-start | bytes 786440 | tf_op jit(solution)/shard_map/while/body/eval_jaxpr/ppermute | solution.py:33
  168.1 14.6 %collective-permute-start.29 = (f32[256,256]{1,0:T(8,128)S(1)}, f32[256,256]{1,0:T(8,128)S(1)}, u32[]{:S(2)}, u32[]{:S(2)}) collective-permute-start(f32[256,256]{1,0:T(8,128)S(1)} %collective-permute-done.25.refs_20_), channel_id=1, source_target_pairs={{0,64},{32,96},{64,128},{96,160},{128,192},{160,224},{192,0},{224,... | collective-permute-start | bytes 786440 | tf_op jit(solution)/shard_map/while/body/eval_jaxpr/ppermute | solution.py:37
  169.8 12.9 %collective-permute-start.27 = (f32[256,256]{1,0:T(8,128)S(1)}, f32[256,256]{1,0:T(8,128)S(1)}, u32[]{:S(2)}, u32[]{:S(2)}) collective-permute-start(f32[256,256]{1,0:T(8,128)S(1)} %collective-permute-done.25.refs_20_), channel_id=1, source_target_pairs={{0,32},{32,0},{64,96},{96,64},{128,160},{160,128},{192,224},{224,1... | collective-permute-start | bytes 786440 | tf_op jit(solution)/shard_map/while/body/eval_jaxpr/ppermute | solution.py:37
  (46 other events, 316.9 us)
where the time goes:
time: 188 us
  waiting for transfers between devices  89.1 us (47%)
  starting transfers between devices  82.8 us (44%)
  Pallas kernels  11.2 us (6%)
  local copies, waits for them, and re-layouts  3.03 us (2%)
    ppermute x36, starting transfers between devices, send(): return lax.ppermute(v, 'col', pairs)  54.9 us
    ppermute x36, waiting for transfers between devices, send(): return lax.ppermute(v, 'col', pairs)  46.5 us
    ppermute x28, waiting for transfers between devices, gather_rows(): move = lambda v, pairs: lax.ppermute(v, 'row', pairs)  42.7 us
    ppermute x28, starting transfers between devices, gather_rows(): move = lambda v, pairs: lax.ppermute(v, 'row', pairs)  27.9 us
    pallas_call x4, Pallas kernels, call(): pl.pallas_call(lambda *refs: body(len(left), len(right), *refs), out_shap...  11.2 us
  transfers between devices with their start and end apart: 64, of which 33 were waited for; matrix products, arithmetic and copies ran while one was open for 0% of the time, Pallas kernels for 0%

commit v1 on v0

--- a/solution.py
+++ b/solution.py
@@ -45,9 +45,10 @@
 
 def row_places(row):
     y, x_lo = row // X_LO, row % X_LO
-    away = jnp.array([0, 0, -1, 1, -1, 1, 2, 2], jnp.int32)
-    beside = jnp.array([0, 1, 0, 0, 1, 1, 0, 1], jnp.int32)
-    return (y + away + Y) % Y * X_LO + (x_lo + beside) % X_LO
+    s = jnp.arange(Y * X_LO, dtype=jnp.int32)
+    away = jnp.where(s < 2, 0, jnp.where(s > 5, 2, 2 * (s % 2) - 1))
+    beside = jnp.where(s < 2, s, jnp.where(s > 5, s % 2, s // 4))
+    return ((y + away + Y) % Y * X_LO + (x_lo + beside) % X_LO) * CORE
 
 
 def gather_cols(tile):
@@ -63,8 +64,10 @@
 
 def col_places(col):
     x_hi, z = col // (Z * CORE), (col // CORE) % Z
-    away = jnp.array([0, 0, -1, 1, -1, 1, -2, 2, -2, 2, -3, 3, -3, 3, 4, 4], jnp.int32)
-    across = jnp.array([0, 1, 0, 0, 1, 1, 0, 0, 1, 1, 0, 0, 1, 1, 0, 1], jnp.int32)
+    s = jnp.arange(X_HI * Z, dtype=jnp.int32)
+    hop = (s + 2) // 4
+    away = jnp.where(s % 2 == 0, -hop, hop)
+    across = jnp.where(hop == 0, s, jnp.where(hop == 4, s - 14, (s + 2) // 2))
     return (x_hi + across) % X_HI * Z + (z + away + Z) % Z
 
 
@@ -83,9 +86,8 @@
 
 
 def partial_product(where, lefts, rights, high, low, total):
-    rows = rights[0].shape[0]
     for j, piece in enumerate(rights):
-        to = pl.ds(pl.multiple_of(where[len(lefts) + j] * rows, BLK), rows)
+        to = pl.ds(pl.multiple_of(where[len(lefts) + j] * BLK, BLK), piece.shape[0])
         high[to, :], low[to, :] = split(piece[...])
     dot = lambda a, b: jnp.dot(a, b, preferred_element_type=jnp.float32)
     for g in range(0, len(lefts), GROUP):
@@ -180,9 +182,11 @@
     where = jnp.concatenate(
         [col_places(col_index), row_places(row_number), core[None]]
     ).astype(jnp.int32)
+
     def purify(_, current):
         left = gather_cols(current)
-        right = gather_rows(to_pair(current, core))
+        pair, left[1] = lax.optimization_barrier((to_pair(current, core), left[1]))
+        right = gather_rows(pair)
         kept, given = call(
             square_body, where, live, left, right, [], (rows_dev // CORE, CORE * BLK)
         )

time: 188 us -> 181 us (0.963)
  waiting for transfers between devices: 89.1 us -> 83.5 us
    ppermute x36, waiting for transfers between devices: 46.5 us -> 43.6 us  [send(): return lax.ppermute(v, 'col', pairs)]
    ppermute x28, waiting for transfers between devices: 42.7 us -> 39.9 us  [gather_rows(): move = lambda v, pairs: lax.ppermute(v, 'row', pairs)]
    ppermute x36, starting transfers between devices: 54.9 us -> 52.6 us  [send(): return lax.ppermute(v, 'col', pairs)]
    ppermute x28, starting transfers between devices: 27.9 us -> 29.7 us  [gather_rows(): move = lambda v, pairs: lax.ppermute(v, 'row', pairs)]
  transfers between devices with their start and end apart: 64 -> 64, of which waited for: 33 -> 30; matrix products, arithmetic and copies ran while one was open for 0% -> 0% of each run, Pallas kernels for 0% -> 0%
where the time goes in v1:
time: 181 us
  waiting for transfers between devices  83.5 us (46%)
  starting transfers between devices  82.3 us (45%)
  Pallas kernels  11.2 us (6%)
    ppermute x36, starting transfers between devices, send(): return lax.ppermute(v, 'col', pairs)  52.6 us
    ppermute x36, waiting for transfers between devices, send(): return lax.ppermute(v, 'col', pairs)  43.6 us
    ppermute x28, waiting for transfers between devices, gather_rows(): move = lambda v, pairs: lax.ppermute(v, 'row', pairs)  39.9 us
    ppermute x28, starting transfers between devices, gather_rows(): move = lambda v, pairs: lax.ppermute(v, 'row', pairs)  29.7 us
    pallas_call x4, Pallas kernels, call(): pl.pallas_call(lambda *refs: body(len(left), len(right), *refs), out_shap...  11.2 us
  transfers between devices with their start and end apart: 64, of which 30 were waited for; matrix products, arithmetic and copies ran while one was open for 0% of the time, Pallas kernels for 0%

profile of v1, /device:TPU:1, one launch (start us, length us, event | category | flops | bytes accessed | tf_op | source)
XLA Modules:
  0.0 180.6 jit_solution(5678900454675880431)
XLA Ops:
  2.5 177.4 %while.12 = (s32[]{:T(128)}, f32[512,128]{1,0:T(8,128)S(1)}, pred[]{:T(512)}, s32[25]{0:T(128)S(1)}, f32[8]{0:T(128)S(1)}, /*index=5*/s32[]{:T(128)}) while((s32[]{:T(128)}, f32[512,128]{1,0:T(8,128)S(1)}, pred[]{:T(512)}, s32[25]{0:T(128)S(1)}, f32[8]{0:T(128)S(1)}, /*index=5*/s32[]{:T(128)}) %tuple.38), condition=%wide.region_2.3_spmd, body=%wide.region_1.2_spmd.sunk | while | flops 3221553152 | bytes 50858308 | solution.py:199
  2.5 3.3 %collective-permute-start = (f32[2,128,128]{2,1,0:T(8,128)S(1)}, f32[2,128,128]{2,1,0:T(8,128)S(1)}, u32[]{:S(2)}, u32[]{:S(2)}) collective-permute-start(f32[2,128,128]{2,1,0:T(8,128)S(1)} %select_bitcast_fusion.2), channel_id=1, source_target_pairs={{0,1},{1,0},{2,3},{3,2},{4,5},{5,4},{6,7},{7,6},{8,9},{9,8},{10,11... | collective-permute-start | bytes 393224 | tf_op jit(solution)/shard_map/while/body/eval_jaxpr/ppermute | solution.py:33
  8.5 3.9 %collective-permute-start.3 = (f32[512,128]{1,0:T(8,128)S(1)}, f32[512,128]{1,0:T(8,128)S(1)}, u32[]{:S(2)}, u32[]{:S(2)}) collective-permute-start(f32[512,128]{1,0:T(8,128)S(1)} %get-tuple-element.156.refs_2_), channel_id=1, source_target_pairs={{0,14},{1,15},{2,0},{3,1},{4,2},{5,3},{6,4},{7,5},{8,6},{9,7},{10,... | collective-permute-start | bytes 786440 | tf_op jit(solution)/shard_map/while/body/eval_jaxpr/ppermute | solution.py:33
  12.5 3.8 %collective-permute-done.2.refs_4_ = f32[512,128]{1,0:T(8,128)S(1)} collective-permute-done((f32[512,128]{1,0:T(8,128)S(1)}, f32[512,128]{1,0:T(8,128)S(1)}, u32[]{:S(2)}, u32[]{:S(2)}) %collective-permute-start.2) | collective-permute-done | bytes 262176 | tf_op jit(solution)/shard_map/while/body/eval_jaxpr/ppermute | solution.py:33
  30.0 2.9 %collective-permute-start.22 = (f32[256,256]{1,0:T(8,128)S(1)}, f32[256,256]{1,0:T(8,128)S(1)}, u32[]{:S(2)}, u32[]{:S(2)}) collective-permute-start(f32[256,256]{1,0:T(8,128)S(1)} %collective-permute-done.16.refs_19_), channel_id=1, source_target_pairs={{0,128},{32,160},{64,192},{96,224},{128,0},{160,32},{192,64},{224,... | collective-permute-start | bytes 786440 | tf_op jit(solution)/shard_map/while/body/eval_jaxpr/ppermute | solution.py:37
  34.7 3.1 %collective-permute-done.10.refs_12_ = f32[512,128]{1,0:T(8,128)S(1)} collective-permute-done((f32[512,128]{1,0:T(8,128)S(1)}, f32[512,128]{1,0:T(8,128)S(1)}, u32[]{:S(2)}, u32[]{:S(2)}) %collective-permute-start.10) | collective-permute-done | bytes 262176 | tf_op jit(solution)/shard_map/while/body/eval_jaxpr/ppermute | solution.py:33
  49.9 5.5 %collective-permute-done.12.refs_14_ = f32[512,128]{1,0:T(8,128)S(1)} collective-permute-done((f32[512,128]{1,0:T(8,128)S(1)}, f32[512,128]{1,0:T(8,128)S(1)}, u32[]{:S(2)}, u32[]{:S(2)}) %collective-permute-start.12) | collective-permute-done | bytes 262176 | tf_op jit(solution)/shard_map/while/body/eval_jaxpr/ppermute | solution.py:33
  55.5 2.8 %eval_jaxpr.6 = (f32[256,256]{1,0:T(8,128)S(1)}, f32[256,256]{1,0:T(8,128)S(1)}) custom-call(s32[25]{0:T(128)S(1)} %get-tuple-element.164.refs_0_, f32[8]{0:T(128)S(1)} %get-tuple-element.165.refs_1_, f32[512,128]{1,0:T(8,128)S(1)} %get-tuple-element.156.refs_2_, f32[512,128]{1,0:T(8,128)S(1)} %collective-permute-done.1.refs_3_, ...), custom_call_target="tpu_custom_call" | custom-call | flops 1610612736 | bytes 7340032 | tf_op jit(solution)/shard_map/while/body/eval_jaxpr/pallas_call | solution.py:142
  58.3 3.7 %collective-permute-start.23 = (f32[256,256]{1,0:T(8,128)S(1)}, f32[256,256]{1,0:T(8,128)S(1)}, u32[]{:S(2)}, u32[]{:S(2)}) collective-permute-start(f32[256,256]{1,0:T(8,128)S(1)} %get-tuple-element.143.refs_27_), channel_id=1, source_target_pairs={{0,1},{1,0},{2,3},{3,2},{4,5},{5,4},{6,7},{7,6},{8,9},{9,8},{10,11... | collective-permute-start | bytes 786440 | tf_op jit(solution)/shard_map/while/body/eval_jaxpr/ppermute | solution.py:33
  63.2 2.8 %collective-permute-start.26 = (f32[256,256]{1,0:T(8,128)S(1)}, f32[256,256]{1,0:T(8,128)S(1)}, u32[]{:S(2)}, u32[]{:S(2)}) collective-permute-start(f32[256,256]{1,0:T(8,128)S(1)} %add.251.refs_18_), channel_id=1, source_target_pairs={{0,192},{32,224},{64,0},{96,32},{128,64},{160,96},{192,128},{224,1... | collective-permute-start | bytes 786440 | tf_op jit(solution)/shard_map/while/body/eval_jaxpr/ppermute | solution.py:37
  67.2 4.1 %collective-permute-done.26.refs_21_ = f32[256,256]{1,0:T(8,128)S(1)} collective-permute-done((f32[256,256]{1,0:T(8,128)S(1)}, f32[256,256]{1,0:T(8,128)S(1)}, u32[]{:S(2)}, u32[]{:S(2)}) %collective-permute-start.26) | collective-permute-done | bytes 262176 | tf_op jit(solution)/shard_map/while/body/eval_jaxpr/ppermute | solution.py:37
  71.3 3.1 %collective-permute-done.25.refs_20_ = f32[256,256]{1,0:T(8,128)S(1)} collective-permute-done((f32[256,256]{1,0:T(8,128)S(1)}, f32[256,256]{1,0:T(8,128)S(1)}, u32[]{:S(2)}, u32[]{:S(2)}) %collective-permute-start.25) | collective-permute-done | bytes 262176 | tf_op jit(solution)/shard_map/while/body/eval_jaxpr/ppermute | solution.py:37
  77.6 4.6 %collective-permute-done.30.refs_25_ = f32[256,256]{1,0:T(8,128)S(1)} collective-permute-done((f32[256,256]{1,0:T(8,128)S(1)}, f32[256,256]{1,0:T(8,128)S(1)}, u32[]{:S(2)}, u32[]{:S(2)}) %collective-permute-start.30) | collective-permute-done | bytes 262176 | tf_op jit(solution)/shard_map/while/body/eval_jaxpr/ppermute | solution.py:37
  82.2 7.4 %collective-permute-done.29.refs_24_ = f32[256,256]{1,0:T(8,128)S(1)} collective-permute-done((f32[256,256]{1,0:T(8,128)S(1)}, f32[256,256]{1,0:T(8,128)S(1)}, u32[]{:S(2)}, u32[]{:S(2)}) %collective-permute-start.29) | collective-permute-done | bytes 262176 | tf_op jit(solution)/shard_map/while/body/eval_jaxpr/ppermute | solution.py:37
  89.6 2.8 %eval_jaxpr.7 = (f32[512,128]{1,0:T(8,128)S(1)}, f32[512,128]{1,0:T(8,128)S(1)}) custom-call(s32[25]{0:T(128)S(1)} %get-tuple-element.164.refs_0_, f32[8]{0:T(128)S(1)} %get-tuple-element.165.refs_1_, f32[512,128]{1,0:T(8,128)S(1)} %get-tuple-element.156.refs_2_, f32[512,128]{1,0:T(8,128)S(1)} %collective-permute-done.1.refs_3_, ...), custom_call_target="tpu_custom_call" | custom-call | flops 1610612736 | bytes 7340032 | tf_op jit(solution)/shard_map/while/body/eval_jaxpr/pallas_call | solution.py:142
  100.3 3.5 %collective-permute-done.2.refs_4_ = f32[512,128]{1,0:T(8,128)S(1)} collective-permute-done((f32[512,128]{1,0:T(8,128)S(1)}, f32[512,128]{1,0:T(8,128)S(1)}, u32[]{:S(2)}, u32[]{:S(2)}) %collective-permute-start.2) | collective-permute-done | bytes 262176 | tf_op jit(solution)/shard_map/while/body/eval_jaxpr/ppermute | solution.py:33
  120.4 4.2 %collective-permute-done.10.refs_12_ = f32[512,128]{1,0:T(8,128)S(1)} collective-permute-done((f32[512,128]{1,0:T(8,128)S(1)}, f32[512,128]{1,0:T(8,128)S(1)}, u32[]{:S(2)}, u32[]{:S(2)}) %collective-permute-start.10) | collective-permute-done | bytes 262176 | tf_op jit(solution)/shard_map/while/body/eval_jaxpr/ppermute | solution.py:33
  134.0 2.8 %collective-permute-done.11.refs_13_ = f32[512,128]{1,0:T(8,128)S(1)} collective-permute-done((f32[512,128]{1,0:T(8,128)S(1)}, f32[512,128]{1,0:T(8,128)S(1)}, u32[]{:S(2)}, u32[]{:S(2)}) %collective-permute-start.11) | collective-permute-done | bytes 262176 | tf_op jit(solution)/shard_map/while/body/eval_jaxpr/ppermute | solution.py:33
  137.1 5.6 %collective-permute-done.12.refs_14_ = f32[512,128]{1,0:T(8,128)S(1)} collective-permute-done((f32[512,128]{1,0:T(8,128)S(1)}, f32[512,128]{1,0:T(8,128)S(1)}, u32[]{:S(2)}, u32[]{:S(2)}) %collective-permute-start.12) | collective-permute-done | bytes 262176 | tf_op jit(solution)/shard_map/while/body/eval_jaxpr/ppermute | solution.py:33
  142.7 2.8 %eval_jaxpr.6 = (f32[256,256]{1,0:T(8,128)S(1)}, f32[256,256]{1,0:T(8,128)S(1)}) custom-call(s32[25]{0:T(128)S(1)} %get-tuple-element.164.refs_0_, f32[8]{0:T(128)S(1)} %get-tuple-element.165.refs_1_, f32[512,128]{1,0:T(8,128)S(1)} %get-tuple-element.156.refs_2_, f32[512,128]{1,0:T(8,128)S(1)} %collective-permute-done.1.refs_3_, ...), custom_call_target="tpu_custom_call" | custom-call | flops 1610612736 | bytes 7340032 | tf_op jit(solution)/shard_map/while/body/eval_jaxpr/pallas_call | solution.py:142
  145.5 3.6 %collective-permute-start.23 = (f32[256,256]{1,0:T(8,128)S(1)}, f32[256,256]{1,0:T(8,128)S(1)}, u32[]{:S(2)}, u32[]{:S(2)}) collective-permute-start(f32[256,256]{1,0:T(8,128)S(1)} %get-tuple-element.143.refs_27_), channel_id=1, source_target_pairs={{0,1},{1,0},{2,3},{3,2},{4,5},{5,4},{6,7},{7,6},{8,9},{9,8},{10,11... | collective-permute-start | bytes 786440 | tf_op jit(solution)/shard_map/while/body/eval_jaxpr/ppermute | solution.py:33
  153.1 4.8 %collective-permute-done.26.refs_21_ = f32[256,256]{1,0:T(8,128)S(1)} collective-permute-done((f32[256,256]{1,0:T(8,128)S(1)}, f32[256,256]{1,0:T(8,128)S(1)}, u32[]{:S(2)}, u32[]{:S(2)}) %collective-permute-start.26) | collective-permute-done | bytes 262176 | tf_op jit(solution)/shard_map/while/body/eval_jaxpr/ppermute | solution.py:37
  163.2 4.6 %collective-permute-done.30.refs_25_ = f32[256,256]{1,0:T(8,128)S(1)} collective-permute-done((f32[256,256]{1,0:T(8,128)S(1)}, f32[256,256]{1,0:T(8,128)S(1)}, u32[]{:S(2)}, u32[]{:S(2)}) %collective-permute-start.30) | collective-permute-done | bytes 262176 | tf_op jit(solution)/shard_map/while/body/eval_jaxpr/ppermute | solution.py:37
  167.8 7.4 %collective-permute-done.29.refs_24_ = f32[256,256]{1,0:T(8,128)S(1)} collective-permute-done((f32[256,256]{1,0:T(8,128)S(1)}, f32[256,256]{1,0:T(8,128)S(1)}, u32[]{:S(2)}, u32[]{:S(2)}) %collective-permute-start.29) | collective-permute-done | bytes 262176 | tf_op jit(solution)/shard_map/while/body/eval_jaxpr/ppermute | solution.py:37
  (138 shorter events, 87.3 us)
Async XLA Ops:
  2.5 9.9 %collective-permute-start = (f32[2,128,128]{2,1,0:T(8,128)S(1)}, f32[2,128,128]{2,1,0:T(8,128)S(1)}, u32[]{:S(2)}, u32[]{:S(2)}) collective-permute-start(f32[2,128,128]{2,1,0:T(8,128)S(1)} %select_bitcast_fusion.2), channel_id=1, source_target_pairs={{0,1},{1,0},{2,3},{3,2},{4,5},{5,4},{6,7},{7,6},{8,9},{9,8},{10,11... | collective-permute-start | bytes 393224 | tf_op jit(solution)/shard_map/while/body/eval_jaxpr/ppermute | solution.py:33
  5.9 10.4 %collective-permute-start.2 = (f32[512,128]{1,0:T(8,128)S(1)}, f32[512,128]{1,0:T(8,128)S(1)}, u32[]{:S(2)}, u32[]{:S(2)}) collective-permute-start(f32[512,128]{1,0:T(8,128)S(1)} %get-tuple-element.156.refs_2_), channel_id=1, source_target_pairs={{0,2},{1,3},{2,4},{3,5},{4,6},{5,7},{6,8},{7,9},{8,10},{9,11},{10,... | collective-permute-start | bytes 786440 | tf_op jit(solution)/shard_map/while/body/eval_jaxpr/ppermute | solution.py:33
  5.9 10.4 %collective-permute-start.1 = (f32[512,128]{1,0:T(8,128)S(1)}, f32[512,128]{1,0:T(8,128)S(1)}, u32[]{:S(2)}, u32[]{:S(2)}) collective-permute-start(f32[512,128]{1,0:T(8,128)S(1)} %get-tuple-element.156.refs_2_), channel_id=1, source_target_pairs={{0,16},{1,17},{2,18},{3,19},{4,20},{5,21},{6,22},{7,23},{8,24},{9,... | collective-permute-start | bytes 786440 | tf_op jit(solution)/shard_map/while/body/eval_jaxpr/ppermute | solution.py:33
  8.5 13.2 %collective-permute-start.3 = (f32[512,128]{1,0:T(8,128)S(1)}, f32[512,128]{1,0:T(8,128)S(1)}, u32[]{:S(2)}, u32[]{:S(2)}) collective-permute-start(f32[512,128]{1,0:T(8,128)S(1)} %get-tuple-element.156.refs_2_), channel_id=1, source_target_pairs={{0,14},{1,15},{2,0},{3,1},{4,2},{5,3},{6,4},{7,5},{8,6},{9,7},{10,... | collective-permute-start | bytes 786440 | tf_op jit(solution)/shard_map/while/body/eval_jaxpr/ppermute | solution.py:33
  24.7 9.5 %collective-permute-start.7 = (f32[512,128]{1,0:T(8,128)S(1)}, f32[512,128]{1,0:T(8,128)S(1)}, u32[]{:S(2)}, u32[]{:S(2)}) collective-permute-start(f32[512,128]{1,0:T(8,128)S(1)} %collective-permute-done.3.refs_5_), channel_id=1, source_target_pairs={{0,14},{1,15},{2,0},{3,1},{4,2},{5,3},{6,4},{7,5},{8,6},{9,7},{10,... | collective-permute-start | bytes 786440 | tf_op jit(solution)/shard_map/while/body/eval_jaxpr/ppermute | solution.py:33
  27.4 10.4 %collective-permute-start.10 = (f32[512,128]{1,0:T(8,128)S(1)}, f32[512,128]{1,0:T(8,128)S(1)}, u32[]{:S(2)}, u32[]{:S(2)}) collective-permute-start(f32[512,128]{1,0:T(8,128)S(1)} %collective-permute-done.6.refs_8_), channel_id=1, source_target_pairs={{0,2},{1,3},{2,4},{3,5},{4,6},{5,7},{6,8},{7,9},{8,10},{9,11},{10,... | collective-permute-start | bytes 786440 | tf_op jit(solution)/shard_map/while/body/eval_jaxpr/ppermute | solution.py:33
  27.4 10.4 %collective-permute-start.9 = (f32[512,128]{1,0:T(8,128)S(1)}, f32[512,128]{1,0:T(8,128)S(1)}, u32[]{:S(2)}, u32[]{:S(2)}) collective-permute-start(f32[512,128]{1,0:T(8,128)S(1)} %collective-permute-done.5.refs_7_), channel_id=1, source_target_pairs={{0,14},{1,15},{2,0},{3,1},{4,2},{5,3},{6,4},{7,5},{8,6},{9,7},{10,... | collective-permute-start | bytes 786440 | tf_op jit(solution)/shard_map/while/body/eval_jaxpr/ppermute | solution.py:33
  30.0 10.4 %collective-permute-start.22 = (f32[256,256]{1,0:T(8,128)S(1)}, f32[256,256]{1,0:T(8,128)S(1)}, u32[]{:S(2)}, u32[]{:S(2)}) collective-permute-start(f32[256,256]{1,0:T(8,128)S(1)} %collective-permute-done.16.refs_19_), channel_id=1, source_target_pairs={{0,128},{32,160},{64,192},{96,224},{128,0},{160,32},{192,64},{224,... | collective-permute-start | bytes 786440 | tf_op jit(solution)/shard_map/while/body/eval_jaxpr/ppermute | solution.py:37
  44.5 10.9 %collective-permute-start.12 = (f32[512,128]{1,0:T(8,128)S(1)}, f32[512,128]{1,0:T(8,128)S(1)}, u32[]{:S(2)}, u32[]{:S(2)}) collective-permute-start(f32[512,128]{1,0:T(8,128)S(1)} %collective-permute-done.8.refs_10_), channel_id=1, source_target_pairs={{0,2},{1,3},{2,4},{3,5},{4,6},{5,7},{6,8},{7,9},{8,10},{9,11},{10,... | collective-permute-start | bytes 786440 | tf_op jit(solution)/shard_map/while/body/eval_jaxpr/ppermute | solution.py:33
  44.5 11.0 %collective-permute-start.15 = (f32[512,128]{1,0:T(8,128)S(1)}, f32[512,128]{1,0:T(8,128)S(1)}, u32[]{:S(2)}, u32[]{:S(2)}) collective-permute-start(f32[512,128]{1,0:T(8,128)S(1)} %collective-permute-done.13.refs_15_), channel_id=1, source_target_pairs={{0,14},{1,15},{2,0},{3,1},{4,2},{5,3},{6,4},{7,5},{8,6},{9,7},{10,... | collective-permute-start | bytes 786440 | tf_op jit(solution)/shard_map/while/body/eval_jaxpr/ppermute | solution.py:33
  75.8 13.8 %collective-permute-start.29 = (f32[256,256]{1,0:T(8,128)S(1)}, f32[256,256]{1,0:T(8,128)S(1)}, u32[]{:S(2)}, u32[]{:S(2)}) collective-permute-start(f32[256,256]{1,0:T(8,128)S(1)} %collective-permute-done.25.refs_20_), channel_id=1, source_target_pairs={{0,64},{32,96},{64,128},{96,160},{128,192},{160,224},{192,0},{224,... | collective-permute-start | bytes 786440 | tf_op jit(solution)/shard_map/while/body/eval_jaxpr/ppermute | solution.py:37
  77.3 12.3 %collective-permute-start.27 = (f32[256,256]{1,0:T(8,128)S(1)}, f32[256,256]{1,0:T(8,128)S(1)}, u32[]{:S(2)}, u32[]{:S(2)}) collective-permute-start(f32[256,256]{1,0:T(8,128)S(1)} %collective-permute-done.25.refs_20_), channel_id=1, source_target_pairs={{0,32},{32,0},{64,96},{96,64},{128,160},{160,128},{192,224},{224,1... | collective-permute-start | bytes 786440 | tf_op jit(solution)/shard_map/while/body/eval_jaxpr/ppermute | solution.py:37
  94.8 9.2 %collective-permute-start.1 = (f32[512,128]{1,0:T(8,128)S(1)}, f32[512,128]{1,0:T(8,128)S(1)}, u32[]{:S(2)}, u32[]{:S(2)}) collective-permute-start(f32[512,128]{1,0:T(8,128)S(1)} %get-tuple-element.156.refs_2_), channel_id=1, source_target_pairs={{0,16},{1,17},{2,18},{3,19},{4,20},{5,21},{6,22},{7,23},{8,24},{9,... | collective-permute-start | bytes 786440 | tf_op jit(solution)/shard_map/while/body/eval_jaxpr/ppermute | solution.py:33
  97.5 10.4 %collective-permute-start.3 = (f32[512,128]{1,0:T(8,128)S(1)}, f32[512,128]{1,0:T(8,128)S(1)}, u32[]{:S(2)}, u32[]{:S(2)}) collective-permute-start(f32[512,128]{1,0:T(8,128)S(1)} %get-tuple-element.156.refs_2_), channel_id=1, source_target_pairs={{0,14},{1,15},{2,0},{3,1},{4,2},{5,3},{6,4},{7,5},{8,6},{9,7},{10,... | collective-permute-start | bytes 786440 | tf_op jit(solution)/shard_map/while/body/eval_jaxpr/ppermute | solution.py:33
  104.3 10.2 %collective-permute-start.17 = (f32[256,256]{1,0:T(8,128)S(1)}, f32[256,256]{1,0:T(8,128)S(1)}, u32[]{:S(2)}, u32[]{:S(2)}) collective-permute-start(f32[256,256]{1,0:T(8,128)S(1)} %bitcast.51), channel_id=1, source_target_pairs={{0,64},{32,96},{64,128},{96,160},{128,192},{160,224},{192,0},{224,... | collective-permute-start | bytes 786440 | tf_op jit(solution)/shard_map/while/body/eval_jaxpr/ppermute | solution.py:37
  107.9 9.3 %collective-permute-start.16 = (f32[256,256]{1,0:T(8,128)S(1)}, f32[256,256]{1,0:T(8,128)S(1)}, u32[]{:S(2)}, u32[]{:S(2)}) collective-permute-start(f32[256,256]{1,0:T(8,128)S(1)} %bitcast.52), channel_id=1, source_target_pairs={{0,32},{32,0},{64,96},{96,64},{128,160},{160,128},{192,224},{224,1... | collective-permute-start | bytes 786440 | tf_op jit(solution)/shard_map/while/body/eval_jaxpr/ppermute | solution.py:37
  114.5 10.1 %collective-permute-start.10 = (f32[512,128]{1,0:T(8,128)S(1)}, f32[512,128]{1,0:T(8,128)S(1)}, u32[]{:S(2)}, u32[]{:S(2)}) collective-permute-start(f32[512,128]{1,0:T(8,128)S(1)} %collective-permute-done.6.refs_8_), channel_id=1, source_target_pairs={{0,2},{1,3},{2,4},{3,5},{4,6},{5,7},{6,8},{7,9},{8,10},{9,11},{10,... | collective-permute-start | bytes 786440 | tf_op jit(solution)/shard_map/while/body/eval_jaxpr/ppermute | solution.py:33
  114.5 10.1 %collective-permute-start.9 = (f32[512,128]{1,0:T(8,128)S(1)}, f32[512,128]{1,0:T(8,128)S(1)}, u32[]{:S(2)}, u32[]{:S(2)}) collective-permute-start(f32[512,128]{1,0:T(8,128)S(1)} %collective-permute-done.5.refs_7_), channel_id=1, source_target_pairs={{0,14},{1,15},{2,0},{3,1},{4,2},{5,3},{6,4},{7,5},{8,6},{9,7},{10,... | collective-permute-start | bytes 786440 | tf_op jit(solution)/shard_map/while/body/eval_jaxpr/ppermute | solution.py:33
  117.2 10.1 %collective-permute-start.22 = (f32[256,256]{1,0:T(8,128)S(1)}, f32[256,256]{1,0:T(8,128)S(1)}, u32[]{:S(2)}, u32[]{:S(2)}) collective-permute-start(f32[256,256]{1,0:T(8,128)S(1)} %collective-permute-done.16.refs_19_), channel_id=1, source_target_pairs={{0,128},{32,160},{64,192},{96,224},{128,0},{160,32},{192,64},{224,... | collective-permute-start | bytes 786440 | tf_op jit(solution)/shard_map/while/body/eval_jaxpr/ppermute | solution.py:37
  119.0 9.5 %collective-permute-start.20 = (f32[256,256]{1,0:T(8,128)S(1)}, f32[256,256]{1,0:T(8,128)S(1)}, u32[]{:S(2)}, u32[]{:S(2)}) collective-permute-start(f32[256,256]{1,0:T(8,128)S(1)} %collective-permute-done.18.refs_21_), channel_id=1, source_target_pairs={{0,32},{32,0},{64,96},{96,64},{128,160},{160,128},{192,224},{224,1... | collective-permute-start | bytes 786440 | tf_op jit(solution)/shard_map/while/body/eval_jaxpr/ppermute | solution.py:37
  131.3 11.4 %collective-permute-start.12 = (f32[512,128]{1,0:T(8,128)S(1)}, f32[512,128]{1,0:T(8,128)S(1)}, u32[]{:S(2)}, u32[]{:S(2)}) collective-permute-start(f32[512,128]{1,0:T(8,128)S(1)} %collective-permute-done.8.refs_10_), channel_id=1, source_target_pairs={{0,2},{1,3},{2,4},{3,5},{4,6},{5,7},{6,8},{7,9},{8,10},{9,11},{10,... | collective-permute-start | bytes 786440 | tf_op jit(solution)/shard_map/while/body/eval_jaxpr/ppermute | solution.py:33
  131.3 11.4 %collective-permute-start.15 = (f32[512,128]{1,0:T(8,128)S(1)}, f32[512,128]{1,0:T(8,128)S(1)}, u32[]{:S(2)}, u32[]{:S(2)}) collective-permute-start(f32[512,128]{1,0:T(8,128)S(1)} %collective-permute-done.13.refs_15_), channel_id=1, source_target_pairs={{0,14},{1,15},{2,0},{3,1},{4,2},{5,3},{6,4},{7,5},{8,6},{9,7},{10,... | collective-permute-start | bytes 786440 | tf_op jit(solution)/shard_map/while/body/eval_jaxpr/ppermute | solution.py:33
  161.4 13.8 %collective-permute-start.29 = (f32[256,256]{1,0:T(8,128)S(1)}, f32[256,256]{1,0:T(8,128)S(1)}, u32[]{:S(2)}, u32[]{:S(2)}) collective-permute-start(f32[256,256]{1,0:T(8,128)S(1)} %collective-permute-done.25.refs_20_), channel_id=1, source_target_pairs={{0,64},{32,96},{64,128},{96,160},{128,192},{160,224},{192,0},{224,... | collective-permute-start | bytes 786440 | tf_op jit(solution)/shard_map/while/body/eval_jaxpr/ppermute | solution.py:37
  162.1 13.2 %collective-permute-start.27 = (f32[256,256]{1,0:T(8,128)S(1)}, f32[256,256]{1,0:T(8,128)S(1)}, u32[]{:S(2)}, u32[]{:S(2)}) collective-permute-start(f32[256,256]{1,0:T(8,128)S(1)} %collective-permute-done.25.refs_20_), channel_id=1, source_target_pairs={{0,32},{32,0},{64,96},{96,64},{128,160},{160,128},{192,224},{224,1... | collective-permute-start | bytes 786440 | tf_op jit(solution)/shard_map/while/body/eval_jaxpr/ppermute | solution.py:37
  (42 other events, 298.4 us)

commit v2 on v1

--- a/solution.py
+++ b/solution.py
@@ -35,8 +35,8 @@
 
 def gather_rows(tile):
     move = lambda v, pairs: lax.ppermute(v, "row", pairs)
-    first = move(tile, BESIDE), move(tile, NORTH), move(tile, SOUTH)
-    beside, south, north = lax.optimization_barrier(first)
+    north = move(tile, SOUTH)
+    beside, south = lax.optimization_barrier((move(tile, BESIDE), move(tile, NORTH)))
     return [
         tile, beside, south, north,
         move(south, BESIDE), move(north, BESIDE), move(south, NORTH), move(beside, OPPOSITE),

time: 181 us -> 178 us (0.983)
  waiting for transfers between devices: 83.5 us -> 76.5 us
  starting transfers between devices: 82.3 us -> 86.9 us
    ppermute x28, waiting for transfers between devices: 39.9 us -> 33.9 us  [gather_rows(): move = lambda v, pairs: lax.ppermute(v, 'row', pairs)]
    ppermute x28, starting transfers between devices: 29.7 us -> 32.4 us  [gather_rows(): move = lambda v, pairs: lax.ppermute(v, 'row', pairs)]
    ppermute x36, starting transfers between devices: 52.6 us -> 54.6 us  [send(): return lax.ppermute(v, 'col', pairs)]
  transfers between devices with their start and end apart: 64 -> 64, of which waited for: 30 -> 34; matrix products, arithmetic and copies ran while one was open for 0% -> 0% of each run, Pallas kernels for 0% -> 0%
where the time goes in v2:
time: 178 us
  starting transfers between devices  86.9 us (49%)
  waiting for transfers between devices  76.5 us (43%)
  Pallas kernels  11.2 us (6%)
    ppermute x36, starting transfers between devices, send(): return lax.ppermute(v, 'col', pairs)  54.6 us
    ppermute x36, waiting for transfers between devices, send(): return lax.ppermute(v, 'col', pairs)  42.5 us
    ppermute x28, waiting for transfers between devices, gather_rows(): move = lambda v, pairs: lax.ppermute(v, 'row', pairs)  33.9 us
    ppermute x28, starting transfers between devices, gather_rows(): move = lambda v, pairs: lax.ppermute(v, 'row', pairs)  32.4 us
    pallas_call x4, Pallas kernels, call(): pl.pallas_call(lambda *refs: body(len(left), len(right), *refs), out_shap...  11.2 us
  transfers between devices with their start and end apart: 64, of which 34 were waited for; matrix products, arithmetic and copies ran while one was open for 0% of the time, Pallas kernels for 0%

profile of v2, /device:TPU:1, one launch (start us, length us, event | category | flops | bytes accessed | tf_op | source)
XLA Modules:
  0.0 178.2 jit_solution(12753041563171422536)
XLA Ops:
  2.5 175.0 %while.12 = (s32[]{:T(128)}, f32[512,128]{1,0:T(8,128)S(1)}, pred[]{:T(512)}, s32[25]{0:T(128)S(1)}, f32[8]{0:T(128)S(1)}, /*index=5*/s32[]{:T(128)}) while((s32[]{:T(128)}, f32[512,128]{1,0:T(8,128)S(1)}, pred[]{:T(512)}, s32[25]{0:T(128)S(1)}, f32[8]{0:T(128)S(1)}, /*index=5*/s32[]{:T(128)}) %tuple.38), condition=%wide.region_2.3_spmd, body=%wide.region_1.2_spmd.sunk | while | flops 3221553152 | bytes 50858308 | solution.py:199
  2.5 3.3 %collective-permute-start = (f32[2,128,128]{2,1,0:T(8,128)S(1)}, f32[2,128,128]{2,1,0:T(8,128)S(1)}, u32[]{:S(2)}, u32[]{:S(2)}) collective-permute-start(f32[2,128,128]{2,1,0:T(8,128)S(1)} %select_bitcast_fusion.2), channel_id=1, source_target_pairs={{0,1},{1,0},{2,3},{3,2},{4,5},{5,4},{6,7},{7,6},{8,9},{9,8},{10,11... | collective-permute-start | bytes 393224 | tf_op jit(solution)/shard_map/while/body/eval_jaxpr/ppermute | solution.py:33
  8.5 3.9 %collective-permute-start.3 = (f32[512,128]{1,0:T(8,128)S(1)}, f32[512,128]{1,0:T(8,128)S(1)}, u32[]{:S(2)}, u32[]{:S(2)}) collective-permute-start(f32[512,128]{1,0:T(8,128)S(1)} %get-tuple-element.150.refs_2_), channel_id=1, source_target_pairs={{0,14},{1,15},{2,0},{3,1},{4,2},{5,3},{6,4},{7,5},{8,6},{9,7},{10,... | collective-permute-start | bytes 786440 | tf_op jit(solution)/shard_map/while/body/eval_jaxpr/ppermute | solution.py:33
  12.5 3.8 %collective-permute-done.2.refs_4_ = f32[512,128]{1,0:T(8,128)S(1)} collective-permute-done((f32[512,128]{1,0:T(8,128)S(1)}, f32[512,128]{1,0:T(8,128)S(1)}, u32[]{:S(2)}, u32[]{:S(2)}) %collective-permute-start.2) | collective-permute-done | bytes 262176 | tf_op jit(solution)/shard_map/while/body/eval_jaxpr/ppermute | solution.py:33
  32.1 2.9 %collective-permute-start.22 = (f32[256,256]{1,0:T(8,128)S(1)}, f32[256,256]{1,0:T(8,128)S(1)}, u32[]{:S(2)}, u32[]{:S(2)}) collective-permute-start(f32[256,256]{1,0:T(8,128)S(1)} %collective-permute-done.16.refs_19_), channel_id=1, source_target_pairs={{0,128},{32,160},{64,192},{96,224},{128,0},{160,32},{192,64},{224,... | collective-permute-start | bytes 786440 | tf_op jit(solution)/shard_map/while/body/eval_jaxpr/ppermute | solution.py:37
  47.2 2.8 %collective-permute-done.11.refs_13_ = f32[512,128]{1,0:T(8,128)S(1)} collective-permute-done((f32[512,128]{1,0:T(8,128)S(1)}, f32[512,128]{1,0:T(8,128)S(1)}, u32[]{:S(2)}, u32[]{:S(2)}) %collective-permute-start.11) | collective-permute-done | bytes 262176 | tf_op jit(solution)/shard_map/while/body/eval_jaxpr/ppermute | solution.py:33
  50.3 4.0 %collective-permute-done.12.refs_14_ = f32[512,128]{1,0:T(8,128)S(1)} collective-permute-done((f32[512,128]{1,0:T(8,128)S(1)}, f32[512,128]{1,0:T(8,128)S(1)}, u32[]{:S(2)}, u32[]{:S(2)}) %collective-permute-start.12) | collective-permute-done | bytes 262176 | tf_op jit(solution)/shard_map/while/body/eval_jaxpr/ppermute | solution.py:33
  55.5 2.8 %eval_jaxpr.6 = (f32[256,256]{1,0:T(8,128)S(1)}, f32[256,256]{1,0:T(8,128)S(1)}) custom-call(s32[25]{0:T(128)S(1)} %get-tuple-element.158.refs_0_, f32[8]{0:T(128)S(1)} %get-tuple-element.159.refs_1_, f32[512,128]{1,0:T(8,128)S(1)} %get-tuple-element.150.refs_2_, f32[512,128]{1,0:T(8,128)S(1)} %collective-permute-done.1.refs_3_, ...), custom_call_target="tpu_custom_call" | custom-call | flops 1610612736 | bytes 7340032 | tf_op jit(solution)/shard_map/while/body/eval_jaxpr/pallas_call | solution.py:142
  58.4 3.9 %collective-permute-start.23 = (f32[256,256]{1,0:T(8,128)S(1)}, f32[256,256]{1,0:T(8,128)S(1)}, u32[]{:S(2)}, u32[]{:S(2)}) collective-permute-start(f32[256,256]{1,0:T(8,128)S(1)} %get-tuple-element.138.refs_27_), channel_id=1, source_target_pairs={{0,1},{1,0},{2,3},{3,2},{4,5},{5,4},{6,7},{7,6},{8,9},{9,8},{10,11... | collective-permute-start | bytes 786440 | tf_op jit(solution)/shard_map/while/body/eval_jaxpr/ppermute | solution.py:33
  67.4 4.8 %collective-permute-done.25.refs_20_ = f32[256,256]{1,0:T(8,128)S(1)} collective-permute-done((f32[256,256]{1,0:T(8,128)S(1)}, f32[256,256]{1,0:T(8,128)S(1)}, u32[]{:S(2)}, u32[]{:S(2)}) %collective-permute-start.25) | collective-permute-done | bytes 262176 | tf_op jit(solution)/shard_map/while/body/eval_jaxpr/ppermute | solution.py:37
  75.8 4.5 %collective-permute-done.28.refs_23_ = f32[256,256]{1,0:T(8,128)S(1)} collective-permute-done((f32[256,256]{1,0:T(8,128)S(1)}, f32[256,256]{1,0:T(8,128)S(1)}, u32[]{:S(2)}, u32[]{:S(2)}) %collective-permute-start.28) | collective-permute-done | bytes 262176 | tf_op jit(solution)/shard_map/while/body/eval_jaxpr/ppermute | solution.py:37
  80.4 6.5 %collective-permute-done.29.refs_24_ = f32[256,256]{1,0:T(8,128)S(1)} collective-permute-done((f32[256,256]{1,0:T(8,128)S(1)}, f32[256,256]{1,0:T(8,128)S(1)}, u32[]{:S(2)}, u32[]{:S(2)}) %collective-permute-start.29) | collective-permute-done | bytes 262176 | tf_op jit(solution)/shard_map/while/body/eval_jaxpr/ppermute | solution.py:37
  86.9 2.8 %eval_jaxpr.7 = (f32[512,128]{1,0:T(8,128)S(1)}, f32[512,128]{1,0:T(8,128)S(1)}) custom-call(s32[25]{0:T(128)S(1)} %get-tuple-element.158.refs_0_, f32[8]{0:T(128)S(1)} %get-tuple-element.159.refs_1_, f32[512,128]{1,0:T(8,128)S(1)} %get-tuple-element.150.refs_2_, f32[512,128]{1,0:T(8,128)S(1)} %collective-permute-done.1.refs_3_, ...), custom_call_target="tpu_custom_call" | custom-call | flops 1610612736 | bytes 7340032 | tf_op jit(solution)/shard_map/while/body/eval_jaxpr/pallas_call | solution.py:142
  93.2 2.7 %collective-permute-start.1 = (f32[512,128]{1,0:T(8,128)S(1)}, f32[512,128]{1,0:T(8,128)S(1)}, u32[]{:S(2)}, u32[]{:S(2)}) collective-permute-start(f32[512,128]{1,0:T(8,128)S(1)} %get-tuple-element.150.refs_2_), channel_id=1, source_target_pairs={{0,16},{1,17},{2,18},{3,19},{4,20},{5,21},{6,22},{7,23},{8,24},{9,... | collective-permute-start | bytes 786440 | tf_op jit(solution)/shard_map/while/body/eval_jaxpr/ppermute | solution.py:33
  98.7 3.5 %collective-permute-done.2.refs_4_ = f32[512,128]{1,0:T(8,128)S(1)} collective-permute-done((f32[512,128]{1,0:T(8,128)S(1)}, f32[512,128]{1,0:T(8,128)S(1)}, u32[]{:S(2)}, u32[]{:S(2)}) %collective-permute-start.2) | collective-permute-done | bytes 262176 | tf_op jit(solution)/shard_map/while/body/eval_jaxpr/ppermute | solution.py:33
  119.2 3.9 %collective-permute-done.10.refs_12_ = f32[512,128]{1,0:T(8,128)S(1)} collective-permute-done((f32[512,128]{1,0:T(8,128)S(1)}, f32[512,128]{1,0:T(8,128)S(1)}, u32[]{:S(2)}, u32[]{:S(2)}) %collective-permute-start.10) | collective-permute-done | bytes 262176 | tf_op jit(solution)/shard_map/while/body/eval_jaxpr/ppermute | solution.py:33
  132.5 2.8 %collective-permute-done.11.refs_13_ = f32[512,128]{1,0:T(8,128)S(1)} collective-permute-done((f32[512,128]{1,0:T(8,128)S(1)}, f32[512,128]{1,0:T(8,128)S(1)}, u32[]{:S(2)}, u32[]{:S(2)}) %collective-permute-start.11) | collective-permute-done | bytes 262176 | tf_op jit(solution)/shard_map/while/body/eval_jaxpr/ppermute | solution.py:33
  135.5 4.0 %collective-permute-done.12.refs_14_ = f32[512,128]{1,0:T(8,128)S(1)} collective-permute-done((f32[512,128]{1,0:T(8,128)S(1)}, f32[512,128]{1,0:T(8,128)S(1)}, u32[]{:S(2)}, u32[]{:S(2)}) %collective-permute-start.12) | collective-permute-done | bytes 262176 | tf_op jit(solution)/shard_map/while/body/eval_jaxpr/ppermute | solution.py:33
  140.8 2.8 %eval_jaxpr.6 = (f32[256,256]{1,0:T(8,128)S(1)}, f32[256,256]{1,0:T(8,128)S(1)}) custom-call(s32[25]{0:T(128)S(1)} %get-tuple-element.158.refs_0_, f32[8]{0:T(128)S(1)} %get-tuple-element.159.refs_1_, f32[512,128]{1,0:T(8,128)S(1)} %get-tuple-element.150.refs_2_, f32[512,128]{1,0:T(8,128)S(1)} %collective-permute-done.1.refs_3_, ...), custom_call_target="tpu_custom_call" | custom-call | flops 1610612736 | bytes 7340032 | tf_op jit(solution)/shard_map/while/body/eval_jaxpr/pallas_call | solution.py:142
  143.7 3.9 %collective-permute-start.23 = (f32[256,256]{1,0:T(8,128)S(1)}, f32[256,256]{1,0:T(8,128)S(1)}, u32[]{:S(2)}, u32[]{:S(2)}) collective-permute-start(f32[256,256]{1,0:T(8,128)S(1)} %get-tuple-element.138.refs_27_), channel_id=1, source_target_pairs={{0,1},{1,0},{2,3},{3,2},{4,5},{5,4},{6,7},{7,6},{8,9},{9,8},{10,11... | collective-permute-start | bytes 786440 | tf_op jit(solution)/shard_map/while/body/eval_jaxpr/ppermute | solution.py:33
  152.7 4.8 %collective-permute-done.25.refs_20_ = f32[256,256]{1,0:T(8,128)S(1)} collective-permute-done((f32[256,256]{1,0:T(8,128)S(1)}, f32[256,256]{1,0:T(8,128)S(1)}, u32[]{:S(2)}, u32[]{:S(2)}) %collective-permute-start.25) | collective-permute-done | bytes 262176 | tf_op jit(solution)/shard_map/while/body/eval_jaxpr/ppermute | solution.py:37
  160.8 4.0 %collective-permute-done.28.refs_23_ = f32[256,256]{1,0:T(8,128)S(1)} collective-permute-done((f32[256,256]{1,0:T(8,128)S(1)}, f32[256,256]{1,0:T(8,128)S(1)}, u32[]{:S(2)}, u32[]{:S(2)}) %collective-permute-start.28) | collective-permute-done | bytes 262176 | tf_op jit(solution)/shard_map/while/body/eval_jaxpr/ppermute | solution.py:37
  165.7 7.1 %collective-permute-done.29.refs_24_ = f32[256,256]{1,0:T(8,128)S(1)} collective-permute-done((f32[256,256]{1,0:T(8,128)S(1)}, f32[256,256]{1,0:T(8,128)S(1)}, u32[]{:S(2)}, u32[]{:S(2)}) %collective-permute-start.29) | collective-permute-done | bytes 262176 | tf_op jit(solution)/shard_map/while/body/eval_jaxpr/ppermute | solution.py:37
  172.8 2.8 %eval_jaxpr.7 = (f32[512,128]{1,0:T(8,128)S(1)}, f32[512,128]{1,0:T(8,128)S(1)}) custom-call(s32[25]{0:T(128)S(1)} %get-tuple-element.158.refs_0_, f32[8]{0:T(128)S(1)} %get-tuple-element.159.refs_1_, f32[512,128]{1,0:T(8,128)S(1)} %get-tuple-element.150.refs_2_, f32[512,128]{1,0:T(8,128)S(1)} %collective-permute-done.1.refs_3_, ...), custom_call_target="tpu_custom_call" | custom-call | flops 1610612736 | bytes 7340032 | tf_op jit(solution)/shard_map/while/body/eval_jaxpr/pallas_call | solution.py:142
  (138 shorter events, 89.7 us)
Async XLA Ops:
  2.5 9.9 %collective-permute-start = (f32[2,128,128]{2,1,0:T(8,128)S(1)}, f32[2,128,128]{2,1,0:T(8,128)S(1)}, u32[]{:S(2)}, u32[]{:S(2)}) collective-permute-start(f32[2,128,128]{2,1,0:T(8,128)S(1)} %select_bitcast_fusion.2), channel_id=1, source_target_pairs={{0,1},{1,0},{2,3},{3,2},{4,5},{5,4},{6,7},{7,6},{8,9},{9,8},{10,11... | collective-permute-start | bytes 393224 | tf_op jit(solution)/shard_map/while/body/eval_jaxpr/ppermute | solution.py:33
  5.9 10.4 %collective-permute-start.2 = (f32[512,128]{1,0:T(8,128)S(1)}, f32[512,128]{1,0:T(8,128)S(1)}, u32[]{:S(2)}, u32[]{:S(2)}) collective-permute-start(f32[512,128]{1,0:T(8,128)S(1)} %get-tuple-element.150.refs_2_), channel_id=1, source_target_pairs={{0,2},{1,3},{2,4},{3,5},{4,6},{5,7},{6,8},{7,9},{8,10},{9,11},{10,... | collective-permute-start | bytes 786440 | tf_op jit(solution)/shard_map/while/body/eval_jaxpr/ppermute | solution.py:33
  5.9 10.4 %collective-permute-start.1 = (f32[512,128]{1,0:T(8,128)S(1)}, f32[512,128]{1,0:T(8,128)S(1)}, u32[]{:S(2)}, u32[]{:S(2)}) collective-permute-start(f32[512,128]{1,0:T(8,128)S(1)} %get-tuple-element.150.refs_2_), channel_id=1, source_target_pairs={{0,16},{1,17},{2,18},{3,19},{4,20},{5,21},{6,22},{7,23},{8,24},{9,... | collective-permute-start | bytes 786440 | tf_op jit(solution)/shard_map/while/body/eval_jaxpr/ppermute | solution.py:33
  8.5 13.0 %collective-permute-start.3 = (f32[512,128]{1,0:T(8,128)S(1)}, f32[512,128]{1,0:T(8,128)S(1)}, u32[]{:S(2)}, u32[]{:S(2)}) collective-permute-start(f32[512,128]{1,0:T(8,128)S(1)} %get-tuple-element.150.refs_2_), channel_id=1, source_target_pairs={{0,14},{1,15},{2,0},{3,1},{4,2},{5,3},{6,4},{7,5},{8,6},{9,7},{10,... | collective-permute-start | bytes 786440 | tf_op jit(solution)/shard_map/while/body/eval_jaxpr/ppermute | solution.py:33
  17.6 9.8 %collective-permute-start.16 = (f32[256,256]{1,0:T(8,128)S(1)}, f32[256,256]{1,0:T(8,128)S(1)}, u32[]{:S(2)}, u32[]{:S(2)}) collective-permute-start(f32[256,256]{1,0:T(8,128)S(1)} %bitcast.51), channel_id=1, source_target_pairs={{0,32},{32,0},{64,96},{96,64},{128,160},{160,128},{192,224},{224,1... | collective-permute-start | bytes 786440 | tf_op jit(solution)/shard_map/while/body/eval_jaxpr/ppermute | solution.py:37
  24.8 10.2 %collective-permute-start.7 = (f32[512,128]{1,0:T(8,128)S(1)}, f32[512,128]{1,0:T(8,128)S(1)}, u32[]{:S(2)}, u32[]{:S(2)}) collective-permute-start(f32[512,128]{1,0:T(8,128)S(1)} %collective-permute-done.3.refs_5_), channel_id=1, source_target_pairs={{0,14},{1,15},{2,0},{3,1},{4,2},{5,3},{6,4},{7,5},{8,6},{9,7},{10,... | collective-permute-start | bytes 786440 | tf_op jit(solution)/shard_map/while/body/eval_jaxpr/ppermute | solution.py:33
  27.4 10.4 %collective-permute-start.10 = (f32[512,128]{1,0:T(8,128)S(1)}, f32[512,128]{1,0:T(8,128)S(1)}, u32[]{:S(2)}, u32[]{:S(2)}) collective-permute-start(f32[512,128]{1,0:T(8,128)S(1)} %collective-permute-done.6.refs_8_), channel_id=1, source_target_pairs={{0,2},{1,3},{2,4},{3,5},{4,6},{5,7},{6,8},{7,9},{8,10},{9,11},{10,... | collective-permute-start | bytes 786440 | tf_op jit(solution)/shard_map/while/body/eval_jaxpr/ppermute | solution.py:33
  27.4 10.4 %collective-permute-start.9 = (f32[512,128]{1,0:T(8,128)S(1)}, f32[512,128]{1,0:T(8,128)S(1)}, u32[]{:S(2)}, u32[]{:S(2)}) collective-permute-start(f32[512,128]{1,0:T(8,128)S(1)} %collective-permute-done.5.refs_7_), channel_id=1, source_target_pairs={{0,14},{1,15},{2,0},{3,1},{4,2},{5,3},{6,4},{7,5},{8,6},{9,7},{10,... | collective-permute-start | bytes 786440 | tf_op jit(solution)/shard_map/while/body/eval_jaxpr/ppermute | solution.py:33
  30.0 10.4 %collective-permute-start.20 = (f32[256,256]{1,0:T(8,128)S(1)}, f32[256,256]{1,0:T(8,128)S(1)}, u32[]{:S(2)}, u32[]{:S(2)}) collective-permute-start(f32[256,256]{1,0:T(8,128)S(1)} %collective-permute-done.18.refs_21_), channel_id=1, source_target_pairs={{0,32},{32,0},{64,96},{96,64},{128,160},{160,128},{192,224},{224,1... | collective-permute-start | bytes 786440 | tf_op jit(solution)/shard_map/while/body/eval_jaxpr/ppermute | solution.py:37
  32.1 9.5 %collective-permute-start.22 = (f32[256,256]{1,0:T(8,128)S(1)}, f32[256,256]{1,0:T(8,128)S(1)}, u32[]{:S(2)}, u32[]{:S(2)}) collective-permute-start(f32[256,256]{1,0:T(8,128)S(1)} %collective-permute-done.16.refs_19_), channel_id=1, source_target_pairs={{0,128},{32,160},{64,192},{96,224},{128,0},{160,32},{192,64},{224,... | collective-permute-start | bytes 786440 | tf_op jit(solution)/shard_map/while/body/eval_jaxpr/ppermute | solution.py:37
  44.5 9.8 %collective-permute-start.12 = (f32[512,128]{1,0:T(8,128)S(1)}, f32[512,128]{1,0:T(8,128)S(1)}, u32[]{:S(2)}, u32[]{:S(2)}) collective-permute-start(f32[512,128]{1,0:T(8,128)S(1)} %collective-permute-done.8.refs_10_), channel_id=1, source_target_pairs={{0,2},{1,3},{2,4},{3,5},{4,6},{5,7},{6,8},{7,9},{8,10},{9,11},{10,... | collective-permute-start | bytes 786440 | tf_op jit(solution)/shard_map/while/body/eval_jaxpr/ppermute | solution.py:33
  44.5 11.0 %collective-permute-start.15 = (f32[512,128]{1,0:T(8,128)S(1)}, f32[512,128]{1,0:T(8,128)S(1)}, u32[]{:S(2)}, u32[]{:S(2)}) collective-permute-start(f32[512,128]{1,0:T(8,128)S(1)} %collective-permute-done.13.refs_15_), channel_id=1, source_target_pairs={{0,14},{1,15},{2,0},{3,1},{4,2},{5,3},{6,4},{7,5},{8,6},{9,7},{10,... | collective-permute-start | bytes 786440 | tf_op jit(solution)/shard_map/while/body/eval_jaxpr/ppermute | solution.py:33
  75.6 11.3 %collective-permute-start.29 = (f32[256,256]{1,0:T(8,128)S(1)}, f32[256,256]{1,0:T(8,128)S(1)}, u32[]{:S(2)}, u32[]{:S(2)}) collective-permute-start(f32[256,256]{1,0:T(8,128)S(1)} %collective-permute-done.25.refs_20_), channel_id=1, source_target_pairs={{0,64},{32,96},{64,128},{96,160},{128,192},{160,224},{192,0},{224,... | collective-permute-start | bytes 786440 | tf_op jit(solution)/shard_map/while/body/eval_jaxpr/ppermute | solution.py:37
  75.6 11.3 %collective-permute-start.27 = (f32[256,256]{1,0:T(8,128)S(1)}, f32[256,256]{1,0:T(8,128)S(1)}, u32[]{:S(2)}, u32[]{:S(2)}) collective-permute-start(f32[256,256]{1,0:T(8,128)S(1)} %collective-permute-done.25.refs_20_), channel_id=1, source_target_pairs={{0,32},{32,0},{64,96},{96,64},{128,160},{160,128},{192,224},{224,1... | collective-permute-start | bytes 786440 | tf_op jit(solution)/shard_map/while/body/eval_jaxpr/ppermute | solution.py:37
  96.0 10.2 %collective-permute-start.3 = (f32[512,128]{1,0:T(8,128)S(1)}, f32[512,128]{1,0:T(8,128)S(1)}, u32[]{:S(2)}, u32[]{:S(2)}) collective-permute-start(f32[512,128]{1,0:T(8,128)S(1)} %get-tuple-element.150.refs_2_), channel_id=1, source_target_pairs={{0,14},{1,15},{2,0},{3,1},{4,2},{5,3},{6,4},{7,5},{8,6},{9,7},{10,... | collective-permute-start | bytes 786440 | tf_op jit(solution)/shard_map/while/body/eval_jaxpr/ppermute | solution.py:33
  102.5 10.5 %collective-permute-start.16 = (f32[256,256]{1,0:T(8,128)S(1)}, f32[256,256]{1,0:T(8,128)S(1)}, u32[]{:S(2)}, u32[]{:S(2)}) collective-permute-start(f32[256,256]{1,0:T(8,128)S(1)} %bitcast.51), channel_id=1, source_target_pairs={{0,32},{32,0},{64,96},{96,64},{128,160},{160,128},{192,224},{224,1... | collective-permute-start | bytes 786440 | tf_op jit(solution)/shard_map/while/body/eval_jaxpr/ppermute | solution.py:37
  113.0 10.1 %collective-permute-start.10 = (f32[512,128]{1,0:T(8,128)S(1)}, f32[512,128]{1,0:T(8,128)S(1)}, u32[]{:S(2)}, u32[]{:S(2)}) collective-permute-start(f32[512,128]{1,0:T(8,128)S(1)} %collective-permute-done.6.refs_8_), channel_id=1, source_target_pairs={{0,2},{1,3},{2,4},{3,5},{4,6},{5,7},{6,8},{7,9},{8,10},{9,11},{10,... | collective-permute-start | bytes 786440 | tf_op jit(solution)/shard_map/while/body/eval_jaxpr/ppermute | solution.py:33
  113.0 10.1 %collective-permute-start.9 = (f32[512,128]{1,0:T(8,128)S(1)}, f32[512,128]{1,0:T(8,128)S(1)}, u32[]{:S(2)}, u32[]{:S(2)}) collective-permute-start(f32[512,128]{1,0:T(8,128)S(1)} %collective-permute-done.5.refs_7_), channel_id=1, source_target_pairs={{0,14},{1,15},{2,0},{3,1},{4,2},{5,3},{6,4},{7,5},{8,6},{9,7},{10,... | collective-permute-start | bytes 786440 | tf_op jit(solution)/shard_map/while/body/eval_jaxpr/ppermute | solution.py:33
  115.7 10.1 %collective-permute-start.20 = (f32[256,256]{1,0:T(8,128)S(1)}, f32[256,256]{1,0:T(8,128)S(1)}, u32[]{:S(2)}, u32[]{:S(2)}) collective-permute-start(f32[256,256]{1,0:T(8,128)S(1)} %collective-permute-done.18.refs_21_), channel_id=1, source_target_pairs={{0,32},{32,0},{64,96},{96,64},{128,160},{160,128},{192,224},{224,1... | collective-permute-start | bytes 786440 | tf_op jit(solution)/shard_map/while/body/eval_jaxpr/ppermute | solution.py:37
  117.4 9.5 %collective-permute-start.22 = (f32[256,256]{1,0:T(8,128)S(1)}, f32[256,256]{1,0:T(8,128)S(1)}, u32[]{:S(2)}, u32[]{:S(2)}) collective-permute-start(f32[256,256]{1,0:T(8,128)S(1)} %collective-permute-done.16.refs_19_), channel_id=1, source_target_pairs={{0,128},{32,160},{64,192},{96,224},{128,0},{160,32},{192,64},{224,... | collective-permute-start | bytes 786440 | tf_op jit(solution)/shard_map/while/body/eval_jaxpr/ppermute | solution.py:37
  129.8 9.8 %collective-permute-start.12 = (f32[512,128]{1,0:T(8,128)S(1)}, f32[512,128]{1,0:T(8,128)S(1)}, u32[]{:S(2)}, u32[]{:S(2)}) collective-permute-start(f32[512,128]{1,0:T(8,128)S(1)} %collective-permute-done.8.refs_10_), channel_id=1, source_target_pairs={{0,2},{1,3},{2,4},{3,5},{4,6},{5,7},{6,8},{7,9},{8,10},{9,11},{10,... | collective-permute-start | bytes 786440 | tf_op jit(solution)/shard_map/while/body/eval_jaxpr/ppermute | solution.py:33
  129.8 11.0 %collective-permute-start.15 = (f32[512,128]{1,0:T(8,128)S(1)}, f32[512,128]{1,0:T(8,128)S(1)}, u32[]{:S(2)}, u32[]{:S(2)}) collective-permute-start(f32[512,128]{1,0:T(8,128)S(1)} %collective-permute-done.13.refs_15_), channel_id=1, source_target_pairs={{0,14},{1,15},{2,0},{3,1},{4,2},{5,3},{6,4},{7,5},{8,6},{9,7},{10,... | collective-permute-start | bytes 786440 | tf_op jit(solution)/shard_map/while/body/eval_jaxpr/ppermute | solution.py:33
  159.6 13.2 %collective-permute-start.29 = (f32[256,256]{1,0:T(8,128)S(1)}, f32[256,256]{1,0:T(8,128)S(1)}, u32[]{:S(2)}, u32[]{:S(2)}) collective-permute-start(f32[256,256]{1,0:T(8,128)S(1)} %collective-permute-done.25.refs_20_), channel_id=1, source_target_pairs={{0,64},{32,96},{64,128},{96,160},{128,192},{160,224},{192,0},{224,... | collective-permute-start | bytes 786440 | tf_op jit(solution)/shard_map/while/body/eval_jaxpr/ppermute | solution.py:37
  160.5 12.3 %collective-permute-start.27 = (f32[256,256]{1,0:T(8,128)S(1)}, f32[256,256]{1,0:T(8,128)S(1)}, u32[]{:S(2)}, u32[]{:S(2)}) collective-permute-start(f32[256,256]{1,0:T(8,128)S(1)} %collective-permute-done.25.refs_20_), channel_id=1, source_target_pairs={{0,32},{32,0},{64,96},{96,64},{128,160},{160,128},{192,224},{224,1... | collective-permute-start | bytes 786440 | tf_op jit(solution)/shard_map/while/body/eval_jaxpr/ppermute | solution.py:37
  (42 other events, 300.7 us)

commit v3 on v2

--- a/solution.py
+++ b/solution.py
@@ -36,10 +36,12 @@
 def gather_rows(tile):
     move = lambda v, pairs: lax.ppermute(v, "row", pairs)
     north = move(tile, SOUTH)
-    beside, south = lax.optimization_barrier((move(tile, BESIDE), move(tile, NORTH)))
+    next_to = move(tile, BESIDE)
+    opposite = move(next_to, OPPOSITE)
+    beside, south = lax.optimization_barrier((next_to, move(tile, NORTH)))
     return [
         tile, beside, south, north,
-        move(south, BESIDE), move(north, BESIDE), move(south, NORTH), move(beside, OPPOSITE),
+        move(south, BESIDE), move(north, BESIDE), move(south, NORTH), opposite,
     ]
 
 

time: 178 us -> 181 us (1.017)
  starting transfers between devices: 86.9 us -> 95.7 us
  waiting for transfers between devices: 76.5 us -> 70.3 us
    ppermute x28, waiting for transfers between devices: 33.9 us -> 27.7 us  [gather_rows(): move = lambda v, pairs: lax.ppermute(v, 'row', pairs)]
    ppermute x28, starting transfers between devices: 32.4 us -> 37 us  [gather_rows(): move = lambda v, pairs: lax.ppermute(v, 'row', pairs)]
    ppermute x36, starting transfers between devices: 54.6 us -> 58.8 us  [send(): return lax.ppermute(v, 'col', pairs)]
where the time goes in v3:
time: 181 us
  starting transfers between devices  95.7 us (53%)
  waiting for transfers between devices  70.3 us (39%)
  Pallas kernels  11.2 us (6%)
    ppermute x36, starting transfers between devices, send(): return lax.ppermute(v, 'col', pairs)  58.8 us
    ppermute x36, waiting for transfers between devices, send(): return lax.ppermute(v, 'col', pairs)  42.6 us
    ppermute x28, starting transfers between devices, gather_rows(): move = lambda v, pairs: lax.ppermute(v, 'row', pairs)  37 us
    ppermute x28, waiting for transfers between devices, gather_rows(): move = lambda v, pairs: lax.ppermute(v, 'row', pairs)  27.7 us
    pallas_call x4, Pallas kernels, call(): pl.pallas_call(lambda *refs: body(len(left), len(right), *refs), out_shap...  11.2 us
  transfers between devices with their start and end apart: 64, of which 34 were waited for; matrix products, arithmetic and copies ran while one was open for 0% of the time, Pallas kernels for 0%

profile of v3, /device:TPU:1, one launch (start us, length us, event | category | flops | bytes accessed | tf_op | source)
XLA Modules:
  0.0 180.8 jit_solution(1376417713953524407)
XLA Ops:
  2.5 177.6 %while.12 = (s32[]{:T(128)}, f32[512,128]{1,0:T(8,128)S(1)}, pred[]{:T(512)}, s32[25]{0:T(128)S(1)}, f32[8]{0:T(128)S(1)}, /*index=5*/s32[]{:T(128)}) while((s32[]{:T(128)}, f32[512,128]{1,0:T(8,128)S(1)}, pred[]{:T(512)}, s32[25]{0:T(128)S(1)}, f32[8]{0:T(128)S(1)}, /*index=5*/s32[]{:T(128)}) %tuple.38), condition=%wide.region_2.3_spmd, body=%wide.region_1.2_spmd.sunk | while | flops 3221553152 | bytes 50858308 | solution.py:201
  2.5 3.3 %collective-permute-start = (f32[2,128,128]{2,1,0:T(8,128)S(1)}, f32[2,128,128]{2,1,0:T(8,128)S(1)}, u32[]{:S(2)}, u32[]{:S(2)}) collective-permute-start(f32[2,128,128]{2,1,0:T(8,128)S(1)} %select_bitcast_fusion.2), channel_id=1, source_target_pairs={{0,1},{1,0},{2,3},{3,2},{4,5},{5,4},{6,7},{7,6},{8,9},{9,8},{10,11... | collective-permute-start | bytes 393224 | tf_op jit(solution)/shard_map/while/body/eval_jaxpr/ppermute | solution.py:33
  8.5 3.9 %collective-permute-start.3 = (f32[512,128]{1,0:T(8,128)S(1)}, f32[512,128]{1,0:T(8,128)S(1)}, u32[]{:S(2)}, u32[]{:S(2)}) collective-permute-start(f32[512,128]{1,0:T(8,128)S(1)} %get-tuple-element.150.refs_2_), channel_id=1, source_target_pairs={{0,14},{1,15},{2,0},{3,1},{4,2},{5,3},{6,4},{7,5},{8,6},{9,7},{10,... | collective-permute-start | bytes 786440 | tf_op jit(solution)/shard_map/while/body/eval_jaxpr/ppermute | solution.py:33
  12.5 3.8 %collective-permute-done.2.refs_4_ = f32[512,128]{1,0:T(8,128)S(1)} collective-permute-done((f32[512,128]{1,0:T(8,128)S(1)}, f32[512,128]{1,0:T(8,128)S(1)}, u32[]{:S(2)}, u32[]{:S(2)}) %collective-permute-start.2) | collective-permute-done | bytes 262176 | tf_op jit(solution)/shard_map/while/body/eval_jaxpr/ppermute | solution.py:33
  34.7 3.1 %collective-permute-done.10.refs_12_ = f32[512,128]{1,0:T(8,128)S(1)} collective-permute-done((f32[512,128]{1,0:T(8,128)S(1)}, f32[512,128]{1,0:T(8,128)S(1)}, u32[]{:S(2)}, u32[]{:S(2)}) %collective-permute-start.10) | collective-permute-done | bytes 262176 | tf_op jit(solution)/shard_map/while/body/eval_jaxpr/ppermute | solution.py:33
  40.4 2.9 %collective-permute-start.22 = (f32[256,256]{1,0:T(8,128)S(1)}, f32[256,256]{1,0:T(8,128)S(1)}, u32[]{:S(2)}, u32[]{:S(2)}) collective-permute-start(f32[256,256]{1,0:T(8,128)S(1)} %collective-permute-done.16.refs_19_), channel_id=1, source_target_pairs={{0,128},{32,160},{64,192},{96,224},{128,0},{160,32},{192,64},{224,... | collective-permute-start | bytes 786440 | tf_op jit(solution)/shard_map/while/body/eval_jaxpr/ppermute | solution.py:37
  50.2 4.6 %collective-permute-done.12.refs_14_ = f32[512,128]{1,0:T(8,128)S(1)} collective-permute-done((f32[512,128]{1,0:T(8,128)S(1)}, f32[512,128]{1,0:T(8,128)S(1)}, u32[]{:S(2)}, u32[]{:S(2)}) %collective-permute-start.12) | collective-permute-done | bytes 262176 | tf_op jit(solution)/shard_map/while/body/eval_jaxpr/ppermute | solution.py:33
  55.1 2.8 %eval_jaxpr.6 = (f32[256,256]{1,0:T(8,128)S(1)}, f32[256,256]{1,0:T(8,128)S(1)}) custom-call(s32[25]{0:T(128)S(1)} %get-tuple-element.158.refs_0_, f32[8]{0:T(128)S(1)} %get-tuple-element.159.refs_1_, f32[512,128]{1,0:T(8,128)S(1)} %get-tuple-element.150.refs_2_, f32[512,128]{1,0:T(8,128)S(1)} %collective-permute-done.1.refs_3_, ...), custom_call_target="tpu_custom_call" | custom-call | flops 1610612736 | bytes 7340032 | tf_op jit(solution)/shard_map/while/body/eval_jaxpr/pallas_call | solution.py:144
  57.9 4.1 %collective-permute-start.23 = (f32[256,256]{1,0:T(8,128)S(1)}, f32[256,256]{1,0:T(8,128)S(1)}, u32[]{:S(2)}, u32[]{:S(2)}) collective-permute-start(f32[256,256]{1,0:T(8,128)S(1)} %get-tuple-element.138.refs_27_), channel_id=1, source_target_pairs={{0,1},{1,0},{2,3},{3,2},{4,5},{5,4},{6,7},{7,6},{8,9},{9,8},{10,11... | collective-permute-start | bytes 786440 | tf_op jit(solution)/shard_map/while/body/eval_jaxpr/ppermute | solution.py:33
  67.3 4.8 %collective-permute-done.25.refs_20_ = f32[256,256]{1,0:T(8,128)S(1)} collective-permute-done((f32[256,256]{1,0:T(8,128)S(1)}, f32[256,256]{1,0:T(8,128)S(1)}, u32[]{:S(2)}, u32[]{:S(2)}) %collective-permute-start.25) | collective-permute-done | bytes 262176 | tf_op jit(solution)/shard_map/while/body/eval_jaxpr/ppermute | solution.py:37
  75.4 2.8 %collective-permute-start.30 = (f32[256,256]{1,0:T(8,128)S(1)}, f32[256,256]{1,0:T(8,128)S(1)}, u32[]{:S(2)}, u32[]{:S(2)}) collective-permute-start(f32[256,256]{1,0:T(8,128)S(1)} %collective-permute-done.24.refs_19_), channel_id=1, source_target_pairs={{0,128},{32,160},{64,192},{96,224},{128,0},{160,32},{192,64},{224,... | collective-permute-start | bytes 786440 | tf_op jit(solution)/shard_map/while/body/eval_jaxpr/ppermute | solution.py:37
  80.6 3.5 %collective-permute-done.27.refs_22_ = f32[256,256]{1,0:T(8,128)S(1)} collective-permute-done((f32[256,256]{1,0:T(8,128)S(1)}, f32[256,256]{1,0:T(8,128)S(1)}, u32[]{:S(2)}, u32[]{:S(2)}) %collective-permute-start.27) | collective-permute-done | bytes 262176 | tf_op jit(solution)/shard_map/while/body/eval_jaxpr/ppermute | solution.py:37
  87.0 2.8 %eval_jaxpr.7 = (f32[512,128]{1,0:T(8,128)S(1)}, f32[512,128]{1,0:T(8,128)S(1)}) custom-call(s32[25]{0:T(128)S(1)} %get-tuple-element.158.refs_0_, f32[8]{0:T(128)S(1)} %get-tuple-element.159.refs_1_, f32[512,128]{1,0:T(8,128)S(1)} %get-tuple-element.150.refs_2_, f32[512,128]{1,0:T(8,128)S(1)} %collective-permute-done.1.refs_3_, ...), custom_call_target="tpu_custom_call" | custom-call | flops 1610612736 | bytes 7340032 | tf_op jit(solution)/shard_map/while/body/eval_jaxpr/pallas_call | solution.py:144
  89.7 3.0 %collective-permute-start.31 = (f32[512,128]{1,0:T(8,128)S(1)}, f32[512,128]{1,0:T(8,128)S(1)}, u32[]{:S(2)}, u32[]{:S(2)}) collective-permute-start(f32[512,128]{1,0:T(8,128)S(1)} %get-tuple-element.142), channel_id=1, source_target_pairs={{0,1},{1,0},{2,3},{3,2},{4,5},{5,4},{6,7},{7,6},{8,9},{9,8},{10,11... | collective-permute-start | bytes 786440 | tf_op jit(solution)/shard_map/while/body/eval_jaxpr/ppermute | solution.py:33
  99.9 3.5 %collective-permute-done.2.refs_4_ = f32[512,128]{1,0:T(8,128)S(1)} collective-permute-done((f32[512,128]{1,0:T(8,128)S(1)}, f32[512,128]{1,0:T(8,128)S(1)}, u32[]{:S(2)}, u32[]{:S(2)}) %collective-permute-start.2) | collective-permute-done | bytes 262176 | tf_op jit(solution)/shard_map/while/body/eval_jaxpr/ppermute | solution.py:33
  119.8 4.4 %collective-permute-done.10.refs_12_ = f32[512,128]{1,0:T(8,128)S(1)} collective-permute-done((f32[512,128]{1,0:T(8,128)S(1)}, f32[512,128]{1,0:T(8,128)S(1)}, u32[]{:S(2)}, u32[]{:S(2)}) %collective-permute-start.10) | collective-permute-done | bytes 262176 | tf_op jit(solution)/shard_map/while/body/eval_jaxpr/ppermute | solution.py:33
  136.6 5.6 %collective-permute-done.12.refs_14_ = f32[512,128]{1,0:T(8,128)S(1)} collective-permute-done((f32[512,128]{1,0:T(8,128)S(1)}, f32[512,128]{1,0:T(8,128)S(1)}, u32[]{:S(2)}, u32[]{:S(2)}) %collective-permute-start.12) | collective-permute-done | bytes 262176 | tf_op jit(solution)/shard_map/while/body/eval_jaxpr/ppermute | solution.py:33
  142.2 2.8 %eval_jaxpr.6 = (f32[256,256]{1,0:T(8,128)S(1)}, f32[256,256]{1,0:T(8,128)S(1)}) custom-call(s32[25]{0:T(128)S(1)} %get-tuple-element.158.refs_0_, f32[8]{0:T(128)S(1)} %get-tuple-element.159.refs_1_, f32[512,128]{1,0:T(8,128)S(1)} %get-tuple-element.150.refs_2_, f32[512,128]{1,0:T(8,128)S(1)} %collective-permute-done.1.refs_3_, ...), custom_call_target="tpu_custom_call" | custom-call | flops 1610612736 | bytes 7340032 | tf_op jit(solution)/shard_map/while/body/eval_jaxpr/pallas_call | solution.py:144
  145.0 3.5 %collective-permute-start.23 = (f32[256,256]{1,0:T(8,128)S(1)}, f32[256,256]{1,0:T(8,128)S(1)}, u32[]{:S(2)}, u32[]{:S(2)}) collective-permute-start(f32[256,256]{1,0:T(8,128)S(1)} %get-tuple-element.138.refs_27_), channel_id=1, source_target_pairs={{0,1},{1,0},{2,3},{3,2},{4,5},{5,4},{6,7},{7,6},{8,9},{9,8},{10,11... | collective-permute-start | bytes 786440 | tf_op jit(solution)/shard_map/while/body/eval_jaxpr/ppermute | solution.py:33
  153.7 4.8 %collective-permute-done.25.refs_20_ = f32[256,256]{1,0:T(8,128)S(1)} collective-permute-done((f32[256,256]{1,0:T(8,128)S(1)}, f32[256,256]{1,0:T(8,128)S(1)}, u32[]{:S(2)}, u32[]{:S(2)}) %collective-permute-start.25) | collective-permute-done | bytes 262176 | tf_op jit(solution)/shard_map/while/body/eval_jaxpr/ppermute | solution.py:37
  160.0 4.4 %collective-permute-start.30 = (f32[256,256]{1,0:T(8,128)S(1)}, f32[256,256]{1,0:T(8,128)S(1)}, u32[]{:S(2)}, u32[]{:S(2)}) collective-permute-start(f32[256,256]{1,0:T(8,128)S(1)} %collective-permute-done.24.refs_19_), channel_id=1, source_target_pairs={{0,128},{32,160},{64,192},{96,224},{128,0},{160,32},{192,64},{224,... | collective-permute-start | bytes 786440 | tf_op jit(solution)/shard_map/while/body/eval_jaxpr/ppermute | solution.py:37
  167.3 2.9 %collective-permute-done.27.refs_22_ = f32[256,256]{1,0:T(8,128)S(1)} collective-permute-done((f32[256,256]{1,0:T(8,128)S(1)}, f32[256,256]{1,0:T(8,128)S(1)}, u32[]{:S(2)}, u32[]{:S(2)}) %collective-permute-start.27) | collective-permute-done | bytes 262176 | tf_op jit(solution)/shard_map/while/body/eval_jaxpr/ppermute | solution.py:37
  170.2 2.8 %collective-permute-done.30.refs_25_ = f32[256,256]{1,0:T(8,128)S(1)} collective-permute-done((f32[256,256]{1,0:T(8,128)S(1)}, f32[256,256]{1,0:T(8,128)S(1)}, u32[]{:S(2)}, u32[]{:S(2)}) %collective-permute-start.30) | collective-permute-done | bytes 262176 | tf_op jit(solution)/shard_map/while/body/eval_jaxpr/ppermute | solution.py:37
  175.8 3.1 %collective-permute-start.31 = (f32[512,128]{1,0:T(8,128)S(1)}, f32[512,128]{1,0:T(8,128)S(1)}, u32[]{:S(2)}, u32[]{:S(2)}) collective-permute-start(f32[512,128]{1,0:T(8,128)S(1)} %get-tuple-element.142), channel_id=1, source_target_pairs={{0,1},{1,0},{2,3},{3,2},{4,5},{5,4},{6,7},{7,6},{8,9},{9,8},{10,11... | collective-permute-start | bytes 786440 | tf_op jit(solution)/shard_map/while/body/eval_jaxpr/ppermute | solution.py:33
  (138 shorter events, 97.2 us)
Async XLA Ops:
  2.5 9.9 %collective-permute-start = (f32[2,128,128]{2,1,0:T(8,128)S(1)}, f32[2,128,128]{2,1,0:T(8,128)S(1)}, u32[]{:S(2)}, u32[]{:S(2)}) collective-permute-start(f32[2,128,128]{2,1,0:T(8,128)S(1)} %select_bitcast_fusion.2), channel_id=1, source_target_pairs={{0,1},{1,0},{2,3},{3,2},{4,5},{5,4},{6,7},{7,6},{8,9},{9,8},{10,11... | collective-permute-start | bytes 393224 | tf_op jit(solution)/shard_map/while/body/eval_jaxpr/ppermute | solution.py:33
  5.9 10.4 %collective-permute-start.2 = (f32[512,128]{1,0:T(8,128)S(1)}, f32[512,128]{1,0:T(8,128)S(1)}, u32[]{:S(2)}, u32[]{:S(2)}) collective-permute-start(f32[512,128]{1,0:T(8,128)S(1)} %get-tuple-element.150.refs_2_), channel_id=1, source_target_pairs={{0,2},{1,3},{2,4},{3,5},{4,6},{5,7},{6,8},{7,9},{8,10},{9,11},{10,... | collective-permute-start | bytes 786440 | tf_op jit(solution)/shard_map/while/body/eval_jaxpr/ppermute | solution.py:33
  5.9 10.4 %collective-permute-start.1 = (f32[512,128]{1,0:T(8,128)S(1)}, f32[512,128]{1,0:T(8,128)S(1)}, u32[]{:S(2)}, u32[]{:S(2)}) collective-permute-start(f32[512,128]{1,0:T(8,128)S(1)} %get-tuple-element.150.refs_2_), channel_id=1, source_target_pairs={{0,16},{1,17},{2,18},{3,19},{4,20},{5,21},{6,22},{7,23},{8,24},{9,... | collective-permute-start | bytes 786440 | tf_op jit(solution)/shard_map/while/body/eval_jaxpr/ppermute | solution.py:33
  8.5 13.0 %collective-permute-start.3 = (f32[512,128]{1,0:T(8,128)S(1)}, f32[512,128]{1,0:T(8,128)S(1)}, u32[]{:S(2)}, u32[]{:S(2)}) collective-permute-start(f32[512,128]{1,0:T(8,128)S(1)} %get-tuple-element.150.refs_2_), channel_id=1, source_target_pairs={{0,14},{1,15},{2,0},{3,1},{4,2},{5,3},{6,4},{7,5},{8,6},{9,7},{10,... | collective-permute-start | bytes 786440 | tf_op jit(solution)/shard_map/while/body/eval_jaxpr/ppermute | solution.py:33
  17.6 9.8 %collective-permute-start.16 = (f32[256,256]{1,0:T(8,128)S(1)}, f32[256,256]{1,0:T(8,128)S(1)}, u32[]{:S(2)}, u32[]{:S(2)}) collective-permute-start(f32[256,256]{1,0:T(8,128)S(1)} %bitcast.51), channel_id=1, source_target_pairs={{0,32},{32,0},{64,96},{96,64},{128,160},{160,128},{192,224},{224,1... | collective-permute-start | bytes 786440 | tf_op jit(solution)/shard_map/while/body/eval_jaxpr/ppermute | solution.py:37
  27.4 10.4 %collective-permute-start.10 = (f32[512,128]{1,0:T(8,128)S(1)}, f32[512,128]{1,0:T(8,128)S(1)}, u32[]{:S(2)}, u32[]{:S(2)}) collective-permute-start(f32[512,128]{1,0:T(8,128)S(1)} %collective-permute-done.6.refs_8_), channel_id=1, source_target_pairs={{0,2},{1,3},{2,4},{3,5},{4,6},{5,7},{6,8},{7,9},{8,10},{9,11},{10,... | collective-permute-start | bytes 786440 | tf_op jit(solution)/shard_map/while/body/eval_jaxpr/ppermute | solution.py:33
  27.4 10.4 %collective-permute-start.9 = (f32[512,128]{1,0:T(8,128)S(1)}, f32[512,128]{1,0:T(8,128)S(1)}, u32[]{:S(2)}, u32[]{:S(2)}) collective-permute-start(f32[512,128]{1,0:T(8,128)S(1)} %collective-permute-done.5.refs_7_), channel_id=1, source_target_pairs={{0,14},{1,15},{2,0},{3,1},{4,2},{5,3},{6,4},{7,5},{8,6},{9,7},{10,... | collective-permute-start | bytes 786440 | tf_op jit(solution)/shard_map/while/body/eval_jaxpr/ppermute | solution.py:33
  30.0 10.4 %collective-permute-start.20 = (f32[256,256]{1,0:T(8,128)S(1)}, f32[256,256]{1,0:T(8,128)S(1)}, u32[]{:S(2)}, u32[]{:S(2)}) collective-permute-start(f32[256,256]{1,0:T(8,128)S(1)} %collective-permute-done.18.refs_21_), channel_id=1, source_target_pairs={{0,32},{32,0},{64,96},{96,64},{128,160},{160,128},{192,224},{224,1... | collective-permute-start | bytes 786440 | tf_op jit(solution)/shard_map/while/body/eval_jaxpr/ppermute | solution.py:37
  32.1 11.2 %collective-permute-start.21 = (f32[256,256]{1,0:T(8,128)S(1)}, f32[256,256]{1,0:T(8,128)S(1)}, u32[]{:S(2)}, u32[]{:S(2)}) collective-permute-start(f32[256,256]{1,0:T(8,128)S(1)} %collective-permute-done.17.refs_20_), channel_id=1, source_target_pairs={{0,64},{32,96},{64,128},{96,160},{128,192},{160,224},{192,0},{224,... | collective-permute-start | bytes 786440 | tf_op jit(solution)/shard_map/while/body/eval_jaxpr/ppermute | solution.py:37
  33.4 10.1 %collective-permute-start.19 = (f32[256,256]{1,0:T(8,128)S(1)}, f32[256,256]{1,0:T(8,128)S(1)}, u32[]{:S(2)}, u32[]{:S(2)}) collective-permute-start(f32[256,256]{1,0:T(8,128)S(1)} %collective-permute-done.17.refs_20_), channel_id=1, source_target_pairs={{0,32},{32,0},{64,96},{96,64},{128,160},{160,128},{192,224},{224,1... | collective-permute-start | bytes 786440 | tf_op jit(solution)/shard_map/while/body/eval_jaxpr/ppermute | solution.py:37
  44.8 10.0 %collective-permute-start.12 = (f32[512,128]{1,0:T(8,128)S(1)}, f32[512,128]{1,0:T(8,128)S(1)}, u32[]{:S(2)}, u32[]{:S(2)}) collective-permute-start(f32[512,128]{1,0:T(8,128)S(1)} %collective-permute-done.8.refs_10_), channel_id=1, source_target_pairs={{0,2},{1,3},{2,4},{3,5},{4,6},{5,7},{6,8},{7,9},{8,10},{9,11},{10,... | collective-permute-start | bytes 786440 | tf_op jit(solution)/shard_map/while/body/eval_jaxpr/ppermute | solution.py:33
  44.9 10.2 %collective-permute-start.15 = (f32[512,128]{1,0:T(8,128)S(1)}, f32[512,128]{1,0:T(8,128)S(1)}, u32[]{:S(2)}, u32[]{:S(2)}) collective-permute-start(f32[512,128]{1,0:T(8,128)S(1)} %collective-permute-done.13.refs_15_), channel_id=1, source_target_pairs={{0,14},{1,15},{2,0},{3,1},{4,2},{5,3},{6,4},{7,5},{8,6},{9,7},{10,... | collective-permute-start | bytes 786440 | tf_op jit(solution)/shard_map/while/body/eval_jaxpr/ppermute | solution.py:33
  74.2 9.9 %collective-permute-start.27 = (f32[256,256]{1,0:T(8,128)S(1)}, f32[256,256]{1,0:T(8,128)S(1)}, u32[]{:S(2)}, u32[]{:S(2)}) collective-permute-start(f32[256,256]{1,0:T(8,128)S(1)} %collective-permute-done.25.refs_20_), channel_id=1, source_target_pairs={{0,32},{32,0},{64,96},{96,64},{128,160},{160,128},{192,224},{224,1... | collective-permute-start | bytes 786440 | tf_op jit(solution)/shard_map/while/body/eval_jaxpr/ppermute | solution.py:37
  75.4 11.6 %collective-permute-start.30 = (f32[256,256]{1,0:T(8,128)S(1)}, f32[256,256]{1,0:T(8,128)S(1)}, u32[]{:S(2)}, u32[]{:S(2)}) collective-permute-start(f32[256,256]{1,0:T(8,128)S(1)} %collective-permute-done.24.refs_19_), channel_id=1, source_target_pairs={{0,128},{32,160},{64,192},{96,224},{128,0},{160,32},{192,64},{224,... | collective-permute-start | bytes 786440 | tf_op jit(solution)/shard_map/while/body/eval_jaxpr/ppermute | solution.py:37
  97.1 10.2 %collective-permute-start.3 = (f32[512,128]{1,0:T(8,128)S(1)}, f32[512,128]{1,0:T(8,128)S(1)}, u32[]{:S(2)}, u32[]{:S(2)}) collective-permute-start(f32[512,128]{1,0:T(8,128)S(1)} %get-tuple-element.150.refs_2_), channel_id=1, source_target_pairs={{0,14},{1,15},{2,0},{3,1},{4,2},{5,3},{6,4},{7,5},{8,6},{9,7},{10,... | collective-permute-start | bytes 786440 | tf_op jit(solution)/shard_map/while/body/eval_jaxpr/ppermute | solution.py:33
  103.5 10.6 %collective-permute-start.16 = (f32[256,256]{1,0:T(8,128)S(1)}, f32[256,256]{1,0:T(8,128)S(1)}, u32[]{:S(2)}, u32[]{:S(2)}) collective-permute-start(f32[256,256]{1,0:T(8,128)S(1)} %bitcast.51), channel_id=1, source_target_pairs={{0,32},{32,0},{64,96},{96,64},{128,160},{160,128},{192,224},{224,1... | collective-permute-start | bytes 786440 | tf_op jit(solution)/shard_map/while/body/eval_jaxpr/ppermute | solution.py:37
  107.3 9.5 %collective-permute-start.18 = (f32[256,256]{1,0:T(8,128)S(1)}, f32[256,256]{1,0:T(8,128)S(1)}, u32[]{:S(2)}, u32[]{:S(2)}) collective-permute-start(f32[256,256]{1,0:T(8,128)S(1)} %bitcast.52), channel_id=1, source_target_pairs={{0,192},{32,224},{64,0},{96,32},{128,64},{160,96},{192,128},{224,1... | collective-permute-start | bytes 786440 | tf_op jit(solution)/shard_map/while/body/eval_jaxpr/ppermute | solution.py:37
  114.1 10.1 %collective-permute-start.10 = (f32[512,128]{1,0:T(8,128)S(1)}, f32[512,128]{1,0:T(8,128)S(1)}, u32[]{:S(2)}, u32[]{:S(2)}) collective-permute-start(f32[512,128]{1,0:T(8,128)S(1)} %collective-permute-done.6.refs_8_), channel_id=1, source_target_pairs={{0,2},{1,3},{2,4},{3,5},{4,6},{5,7},{6,8},{7,9},{8,10},{9,11},{10,... | collective-permute-start | bytes 786440 | tf_op jit(solution)/shard_map/while/body/eval_jaxpr/ppermute | solution.py:33
  114.1 10.1 %collective-permute-start.9 = (f32[512,128]{1,0:T(8,128)S(1)}, f32[512,128]{1,0:T(8,128)S(1)}, u32[]{:S(2)}, u32[]{:S(2)}) collective-permute-start(f32[512,128]{1,0:T(8,128)S(1)} %collective-permute-done.5.refs_7_), channel_id=1, source_target_pairs={{0,14},{1,15},{2,0},{3,1},{4,2},{5,3},{6,4},{7,5},{8,6},{9,7},{10,... | collective-permute-start | bytes 786440 | tf_op jit(solution)/shard_map/while/body/eval_jaxpr/ppermute | solution.py:33
  116.8 10.1 %collective-permute-start.20 = (f32[256,256]{1,0:T(8,128)S(1)}, f32[256,256]{1,0:T(8,128)S(1)}, u32[]{:S(2)}, u32[]{:S(2)}) collective-permute-start(f32[256,256]{1,0:T(8,128)S(1)} %collective-permute-done.18.refs_21_), channel_id=1, source_target_pairs={{0,32},{32,0},{64,96},{96,64},{128,160},{160,128},{192,224},{224,1... | collective-permute-start | bytes 786440 | tf_op jit(solution)/shard_map/while/body/eval_jaxpr/ppermute | solution.py:37
  130.9 11.3 %collective-permute-start.12 = (f32[512,128]{1,0:T(8,128)S(1)}, f32[512,128]{1,0:T(8,128)S(1)}, u32[]{:S(2)}, u32[]{:S(2)}) collective-permute-start(f32[512,128]{1,0:T(8,128)S(1)} %collective-permute-done.8.refs_10_), channel_id=1, source_target_pairs={{0,2},{1,3},{2,4},{3,5},{4,6},{5,7},{6,8},{7,9},{8,10},{9,11},{10,... | collective-permute-start | bytes 786440 | tf_op jit(solution)/shard_map/while/body/eval_jaxpr/ppermute | solution.py:33
  130.9 11.3 %collective-permute-start.15 = (f32[512,128]{1,0:T(8,128)S(1)}, f32[512,128]{1,0:T(8,128)S(1)}, u32[]{:S(2)}, u32[]{:S(2)}) collective-permute-start(f32[512,128]{1,0:T(8,128)S(1)} %collective-permute-done.13.refs_15_), channel_id=1, source_target_pairs={{0,14},{1,15},{2,0},{3,1},{4,2},{5,3},{6,4},{7,5},{8,6},{9,7},{10,... | collective-permute-start | bytes 786440 | tf_op jit(solution)/shard_map/while/body/eval_jaxpr/ppermute | solution.py:33
  159.8 10.5 %collective-permute-start.27 = (f32[256,256]{1,0:T(8,128)S(1)}, f32[256,256]{1,0:T(8,128)S(1)}, u32[]{:S(2)}, u32[]{:S(2)}) collective-permute-start(f32[256,256]{1,0:T(8,128)S(1)} %collective-permute-done.25.refs_20_), channel_id=1, source_target_pairs={{0,32},{32,0},{64,96},{96,64},{128,160},{160,128},{192,224},{224,1... | collective-permute-start | bytes 786440 | tf_op jit(solution)/shard_map/while/body/eval_jaxpr/ppermute | solution.py:37
  160.0 13.0 %collective-permute-start.30 = (f32[256,256]{1,0:T(8,128)S(1)}, f32[256,256]{1,0:T(8,128)S(1)}, u32[]{:S(2)}, u32[]{:S(2)}) collective-permute-start(f32[256,256]{1,0:T(8,128)S(1)} %collective-permute-done.24.refs_19_), channel_id=1, source_target_pairs={{0,128},{32,160},{64,192},{96,224},{128,0},{160,32},{192,64},{224,... | collective-permute-start | bytes 786440 | tf_op jit(solution)/shard_map/while/body/eval_jaxpr/ppermute | solution.py:37
  (42 other events, 297.5 us)
